TPU v7x, 32 devices: a whole 2x2x4 slice. The times are simulated.
32 devices in a mesh: groups: 2 (over y), seq: 4 (over z), head: 2 (over x), dp: 2 (over core).
Axes of the slice: x: 2, y: 2, z: 4, core: 2. Of those that a mesh axis runs over, the one named last changes fastest.
Arguments:
- x_input: bfloat16 [4, 1024, 5120], P(('groups', 'dp'), 'seq', 'head'), parts along dimension 0, may hold values from -6 to 6
- bc_input: bfloat16 [4, 1024, 256], P(('groups', 'dp'), 'seq'), parts along dimension 0, may hold values from -6 to 6
- decays: float32 [4, 80, 1024], P(('groups', 'dp'), 'head', 'seq'), parts along dimension 0, may hold values from 0.5 to 1, as said below
- conv_x: float32 [4, 5120], P(None, 'head'), may hold values from -3 to 3
- conv_bc: float32 [4, 256], replicated, may hold values from -3 to 3
- skip_gain: float32 [80], P('head'), may hold values from 0.5 to 2
- grad_out: bfloat16 [4, 1024, 5120], P(('groups', 'dp'), 'seq', 'head'), parts along dimension 0, may hold values from -6 to 6
Outputs:
- y_output: bfloat16 [4, 1024, 5120], P(('groups', 'dp'), 'seq', 'head'), parts along dimension 0
- grad_x: bfloat16 [4, 1024, 5120], P(('groups', 'dp'), 'seq', 'head'), parts along dimension 0
- grad_bc: bfloat16 [4, 1024, 256], P(('groups', 'dp'), 'seq'), parts along dimension 0
- grad_conv_x: float32 [8, 5120], P('groups', 'head'), parts along dimension 0
- grad_conv_bc: float32 [8, 256], P('groups'), parts along dimension 0
- grad_skip: float32 [160], P(('groups', 'head')), parts along dimension 0
There are 2 independent parts, one for each index of `groups`. A program takes and returns all parts, laid end to end along the dimension named above; an argument that names none is the same for every part. Nothing has to cross between parts.
Inputs may be any that keep to these rules, and one draw needn't show every extreme that they name: `decays`: every decay is strictly below 1.
All inputs are finite; a program needn't handle non-finite values.
Results may differ from a plain program's by a relative error of at most 0.009.
Values may be sent and summed in bfloat16 or wider, within the bound.
A program may use at most 64 MiB of HBM per device.

v0:
```python
import jax
import jax.numpy as jnp
from jax import lax
from jax.sharding import PartitionSpec as P

BLOCK_LEN = 256


highest = lax.Precision.HIGHEST
triple = lax.Precision.HIGH


def shifted(block, axis, distance):
    devices = range(lax.axis_size(axis))
    route = [(i - distance, i) for i in devices if i - distance in devices]
    return lax.ppermute(block, axis, route)


def carried_in(part, axis, combine, identity, reverse):
    count = lax.axis_size(axis)
    place = lax.axis_index(axis)
    ahead = count - 1 - place if reverse else place
    gathered = jax.tree.map(lambda a: lax.all_gather(a, axis), part)
    state = jax.tree.map(lambda a, e: jnp.zeros_like(a) + jnp.asarray(e, a.dtype), part, identity)

    def one(hop, state):
        source = count - 1 - hop if reverse else hop
        return combine(
            state, jax.tree.map(lambda a: lax.dynamic_index_in_dim(a, source, 0, False), gathered)
        )

    return lax.fori_loop(0, ahead, one, state)


def silu_grad(pre):
    sigma = jax.nn.sigmoid(pre)
    return sigma * (1.0 + pre * (1.0 - sigma))


def conv_forward(padded, weight, length):
    total = jnp.zeros((length, weight.shape[1]), jnp.float32)
    for shift in range(weight.shape[0]):
        total = total + weight[shift][None, :] * padded[shift : shift + length].astype(jnp.float32)
    return total


def conv_backward(padded, weight, length):
    taps = weight.shape[0]
    total = jnp.zeros((length, weight.shape[1]), jnp.float32)
    for shift in range(taps):
        total = (
            total + weight[shift][None, :] * padded[taps - 1 - shift : taps - 1 - shift + length]
        )
    return total


def conv_weight_grad(pregrad, padded, taps):
    length = pregrad.shape[0]
    return jnp.stack(
        [
            jnp.sum(pregrad * padded[shift : shift + length].astype(jnp.float32), axis=0)
            for shift in range(taps)
        ]
    )


def decay_matrix(cum_block):
    size = cum_block.shape[-1]
    rows = jnp.arange(size)
    lower = (rows[:, None] >= rows[None, :])[None]
    diff = cum_block[:, :, None] - cum_block[:, None, :]
    return jnp.where(lower, jnp.exp(jnp.where(lower, diff, 0.0)), 0.0)


def join_pair(earlier, later):
    return (earlier[0] + later[0], jnp.exp(later[0])[:, None, None] * earlier[1] + later[1])


def local(x_input, bc_input, decays, conv_x, conv_bc, skip_gain, grad_out):
    x_rows = x_input[0]
    bc_rows = bc_input[0]
    decay_rows = decays[0]
    grad_rows = grad_out[0]
    tokens = x_rows.shape[0]
    taps = conv_x.shape[0]
    heads = decay_rows.shape[0]
    head_dim = x_rows.shape[1] // heads
    state_dim = bc_rows.shape[1] // 2
    scale = state_dim ** (-0.5)
    blocks = tokens // BLOCK_LEN
    x_prev, bc_prev = shifted((x_rows[tokens - taps + 1 :], bc_rows[tokens - taps + 1 :]), "seq", 1)
    x_pad = jnp.concatenate([x_prev, x_rows], axis=0)
    bc_pad = jnp.concatenate([bc_prev, bc_rows], axis=0)
    pre_x = conv_forward(x_pad, conv_x, tokens)
    pre_bc = conv_forward(bc_pad, conv_bc, tokens)
    inner = jax.nn.silu(pre_x).astype(jnp.bfloat16)
    mapped = jax.nn.silu(pre_bc).astype(jnp.bfloat16)
    b_mat = mapped[:, :state_dim]
    c_mat = mapped[:, state_dim:]
    logarithm_decay = jnp.log(decay_rows)
    input_gain = jnp.sqrt(-jnp.expm1(2.0 * logarithm_decay))
    inner_f = inner.astype(jnp.float32).reshape(tokens, heads, head_dim)
    weighted = (inner_f * input_gain.T[:, :, None]).astype(jnp.bfloat16)
    block_cum = jnp.cumsum(logarithm_decay.reshape(heads, blocks, BLOCK_LEN), axis=-1).transpose(
        1, 0, 2
    )
    w_blocks = weighted.reshape(blocks, BLOCK_LEN, heads, head_dim)
    b_blocks = b_mat.reshape(blocks, BLOCK_LEN, state_dim)
    c_blocks = c_mat.reshape(blocks, BLOCK_LEN, state_dim)
    g_blocks = grad_rows.reshape(blocks, BLOCK_LEN, heads, head_dim)

    def forward_block(state, item):
        cum_b, w_b, b_b, c_b = item
        sim = jnp.dot(c_b, b_b.T, preferred_element_type=jnp.float32)
        mixing = (decay_matrix(cum_b) * sim[None]).astype(jnp.bfloat16)
        intra = jnp.einsum("hij,jhp->ihp", mixing, w_b, preferred_element_type=jnp.float32)
        inter = jnp.exp(cum_b).T[:, :, None] * jnp.einsum(
            "in,hpn->ihp", c_b.astype(jnp.float32), state, precision=triple
        )
        tail = jnp.exp(cum_b[:, -1:] - cum_b)
        update = jnp.einsum(
            "jhp,jn->hpn",
            w_b.astype(jnp.float32) * tail.T[:, :, None],
            b_b.astype(jnp.float32),
            precision=triple,
        )
        return (jnp.exp(cum_b[:, -1])[:, None, None] * state + update, (intra + inter, state))

    zero_state = jnp.zeros((heads, head_dim, state_dim), jnp.float32)
    final_state, (mixed, prior) = lax.scan(
        forward_block, zero_state, (block_cum, w_blocks, b_blocks, c_blocks)
    )

    def backward_block(grad, item):
        cum_b, w_b, b_b, c_b, g_b, prior_b = item
        sim = jnp.dot(c_b, b_b.T, preferred_element_type=jnp.float32)
        decay_b = decay_matrix(cum_b)
        mixing = (decay_b * sim[None]).astype(jnp.bfloat16)
        tail = jnp.exp(cum_b[:, -1:] - cum_b)
        w_f = w_b.astype(jnp.float32)
        d_w = scale * jnp.einsum("hij,ihp->jhp", mixing, g_b, preferred_element_type=jnp.float32)
        d_w = d_w + tail.T[:, :, None] * jnp.einsum(
            "jn,hpn->jhp", b_b.astype(jnp.float32), grad, precision=triple
        )
        d_mix = scale * jnp.einsum("ihp,jhp->hij", g_b, w_b, preferred_element_type=jnp.float32)
        d_sim = jnp.sum(d_mix * decay_b, axis=0)
        lead = scale * g_b.astype(jnp.float32) * jnp.exp(cum_b).T[:, :, None]
        d_c = jnp.dot(d_sim, b_b.astype(jnp.float32), precision=highest)
        d_c = d_c + jnp.einsum("ihp,hpn->in", lead, prior_b, precision=triple)
        d_b = jnp.dot(d_sim.T, c_b.astype(jnp.float32), precision=highest)
        d_b = d_b + jnp.einsum("jhp,hpn->jn", w_f * tail.T[:, :, None], grad, precision=triple)
        new_grad = jnp.exp(cum_b[:, -1])[:, None, None] * grad + jnp.einsum(
            "ihp,in->hpn", lead, c_b.astype(jnp.float32), precision=triple
        )
        return (new_grad, (d_w, d_b, d_c))

    start_grad, (d_weighted, d_bmat, d_cmat) = lax.scan(
        backward_block,
        zero_state,
        (block_cum, w_blocks, b_blocks, c_blocks, g_blocks, prior),
        reverse=True,
    )
    totals = jnp.sum(logarithm_decay, axis=1)
    zero_totals = jnp.zeros((heads,), jnp.float32)
    incoming = carried_in(
        (totals, final_state), "seq", join_pair, (zero_totals, zero_state), False
    )[1]
    outgoing = carried_in((totals, start_grad), "seq", join_pair, (zero_totals, zero_state), True)[
        1
    ]
    run_decay = jnp.cumsum(logarithm_decay, axis=1)
    lead_factor = jnp.exp(run_decay).T[:, :, None]
    tail_factor = jnp.exp(run_decay[:, -1:] - run_decay).T[:, :, None]
    b_f = b_mat.astype(jnp.float32)
    c_f = c_mat.astype(jnp.float32)
    grad_f = grad_rows.astype(jnp.float32).reshape(tokens, heads, head_dim)
    y_extra = lead_factor * jnp.einsum("tn,hpn->thp", c_f, incoming, precision=triple)
    skip_rep = jnp.repeat(skip_gain, head_dim)[None, :]
    y_sum = scale * (mixed.reshape(tokens, heads, head_dim) + y_extra)
    y_rows = (
        y_sum.reshape(tokens, heads * head_dim) + skip_rep * inner.astype(jnp.float32)
    ).astype(jnp.bfloat16)
    d_w_all = d_weighted.reshape(tokens, heads, head_dim) + tail_factor * jnp.einsum(
        "tn,hpn->thp", b_f, outgoing, precision=triple
    )
    w_tail = weighted.astype(jnp.float32) * tail_factor
    d_b_all = d_bmat.reshape(tokens, state_dim) + jnp.einsum(
        "thp,hpn->tn", w_tail, outgoing, precision=triple
    )
    d_c_all = d_cmat.reshape(tokens, state_dim) + jnp.einsum(
        "thp,hpn->tn", scale * grad_f * lead_factor, incoming, precision=triple
    )
    d_local = jnp.concatenate([d_b_all, d_c_all], axis=1)
    d_inner = (input_gain.T[:, :, None] * d_w_all).reshape(
        tokens, heads * head_dim
    ) + skip_rep * grad_rows.astype(jnp.float32)
    d_pre_x = d_inner * silu_grad(pre_x)
    share = 2 * state_dim // lax.axis_size("head")
    offset = lax.axis_index("head") * share
    d_local_t = d_local.T
    d_share = lax.psum_scatter(d_local_t, "head", scatter_dimension=0, tiled=True).T
    pre_part = lax.dynamic_slice_in_dim(pre_bc, offset, share, 1)
    taps_part = lax.dynamic_slice_in_dim(conv_bc, offset, share, 1)
    pad_part = lax.dynamic_slice_in_dim(bc_pad, offset, share, 1)
    d_pre_bc = d_share * silu_grad(pre_part)
    next_x, next_bc = shifted((d_pre_x[: taps - 1], d_pre_bc[: taps - 1]), "seq", -1)
    grad_x_rows = conv_backward(jnp.concatenate([d_pre_x, next_x], axis=0), conv_x, tokens).astype(
        jnp.bfloat16
    )
    grad_bc_part = conv_backward(
        jnp.concatenate([d_pre_bc, next_bc], axis=0), taps_part, tokens
    ).astype(jnp.bfloat16)
    taps_x = conv_weight_grad(d_pre_x, x_pad, taps)
    taps_bc_part = conv_weight_grad(d_pre_bc, pad_part, taps)
    grad_bc_rows = lax.all_gather(grad_bc_part, "head", axis=1, tiled=True)
    taps_bc = lax.all_gather(taps_bc_part, "head", axis=1, tiled=True)
    skip_term = jnp.sum(grad_f * inner_f, axis=(0, 2))
    sum_x, sum_bc, sum_skip = lax.psum((taps_x, taps_bc, skip_term), ("seq", "dp"))
    token_count = tokens * lax.axis_size("seq") * lax.axis_size("dp")
    norm_tokens = float(token_count) ** (-0.5)
    norm_skip = float(token_count * head_dim) ** (-0.5)
    return (
        y_rows[None],
        grad_x_rows[None],
        grad_bc_rows[None],
        sum_x * norm_tokens,
        sum_bc * norm_tokens,
        sum_skip * norm_skip,
    )


def solution(mesh):
    return jax.shard_map(
        local,
        mesh=mesh,
        in_specs=(
            P(("groups", "dp"), "seq", "head"),
            P(("groups", "dp"), "seq", None),
            P(("groups", "dp"), "head", "seq"),
            P(None, "head"),
            P(),
            P("head"),
            P(("groups", "dp"), "seq", "head"),
        ),
        out_specs=(
            P(("groups", "dp"), "seq", "head"),
            P(("groups", "dp"), "seq", "head"),
            P(("groups", "dp"), "seq", None),
            P("groups", "head"),
            P("groups", None),
            P(("groups", "head")),
        ),
        check_vma=False,
    )
```

profile of v0, /device:TPU:0, one launch (start us, length us, event | category | flops | bytes accessed | tf_op | source)
XLA Modules:
  0.0 329.8 jit_solution(5727681315043839589)
XLA Ops:
  7.9 4.9 %collective-permute-start.1 = (bf16[3,256]{1,0:T(4,128)(2,1)S(1)}, bf16[3,256]{1,0:T(4,128)(2,1)S(1)}, u32[]{:S(2)}, u32[]{:S(2)}) collective-permute-start(bf16[3,256]{1,0:T(4,128)(2,1)S(1)} %slice_bitcast_fusion.1), channel_id=1, source_target_pairs={{0,4},{4,8},{8,12},{1,5},{5,9},{9,13},{2,6},{6,10},{10,14},{3,7},{... | collective-permute-start | bytes 4616 | tf_op jit(solution)/shard_map/ppermute | solution.py:16
  17.8 1.9 fusion.32
  19.8 3.5 %collective-permute-start = (bf16[3,2560]{1,0:T(4,128)(2,1)S(1)}, bf16[3,2560]{1,0:T(4,128)(2,1)S(1)}, u32[]{:S(2)}, u32[]{:S(2)}) collective-permute-start(bf16[3,2560]{1,0:T(4,128)(2,1)S(1)} %slice_bitcast_fusion), channel_id=1, source_target_pairs={{0,4},{4,8},{8,12},{1,5},{5,9},{9,13},{2,6},{6,10},{10,14},{3,7},{... | collective-permute-start | bytes 46088 | tf_op jit(solution)/shard_map/ppermute | solution.py:16
  24.9 10.1 %all-reduce = f32[160]{0:T(256)S(1)} all-reduce(f32[160]{0:T(256)S(1)} %dynamic-update-slice), channel_id=2, replica_groups=mesh['groups'=2,'seq'=4,'head'=2,'dp'=2] {'seq'}, use_global_device_ids=true, to_apply=%add | all-reduce | flops 160 | bytes 1280
  38.5 2.4 fusion.53
  40.9 4.7 %fusion.1 = f32[40,256,64]{1,2,0:T(8,128)} fusion(bf16[256,40,64]{0,2,1:T(8,128)(2,1)S(1)} %bitcast.154, f32[256,256]{0,1:T(8,128)S(1)} %fusion.81, f32[40,256]{1,0:T(8,128)S(1)} %get-tuple-element.233, pred[256,256]{0,1:T(8,128)(4,1)S(1)} %iota_compare_fusion), kind=kOutput, calls=%fused_computation.8 | convolution fusion | flops 348651520 | bytes 4300800 | tf_op jit(solution)/shard_map/while/body/eval_jaxpr/hij,ihp->jhp/dot_general | solution.py:141
  45.6 72.7 %all-gather.8.cloned.1.call-done = f32[160,64,128]{2,1,0:T(8,128)} async-done(((f32[40,64,128]{2,1,0:T(8,128)}), f32[160,64,128]{2,1,0:T(8,128)}) %all-gather.8.cloned.1.call-update) | async-done | bytes 5242896 | tf_op jit(solution)/shard_map/all_gather | solution.py:23
  118.4 6.9 %while.17 = (s32[]{:T(128)}, f32[40,64,128]{2,1,0:T(8,128)S(1)}, s32[]{:T(128)}, f32[4,40]{1,0:T(4,128)}, f32[4,40,64,128]{3,2,1,0:T(8,128)}, /*index=5*/s32[]{:T(128)}, s32[]{:T(128)}, s32[]{:T(128)}, s32[]{:T(128)}) while((s32[]{:T(128)}, f32[40,64,128]{2,1,0:T(8,128)S(1)}, s32[]{:T(128)}, f32[4,40]{1,0:T(4,128)}, ...), condition=%wide.region_8.9_spmd, body=%wide.region_7.8_spmd.sunk | while | flops 655366 | bytes 3932787 | solution.py:32
  125.3 5.1 %fusion.29 = f32[256,40,64]{0,2,1:T(8,128)} fusion(f32[256,40,64]{0,2,1:T(8,128)} %fusion.53, f32[40,256,64]{1,2,0:T(8,128)} %fusion.1, f32[40,64,128]{2,1,0:T(8,128)S(1)} %get-tuple-element.192, f32[256,40]{0,1:T(8,128)S(1)} %get-tuple-element.237, f32[256,40]{0,1:T(8,128)S(1)} %get-tuple-element.240, f32[256,40]{0,1:T(8,128)S(1)} %get-tuple-element.242, ...), kind=kOutput, calls=%fused_computation.54 | convolution fusion | flops 507248640 | bytes 9363456 | tf_op jit(solution)/shard_map/tn,hpn->thp/dot_general | solution.py:183
  130.4 3.2 copy.103
  133.7 5.1 %fusion.10 = (f32[2560]{0:T(1024)S(1)}, f32[2560]{0:T(1024)S(1)}, f32[2560]{0:T(1024)S(1)}, f32[2560]{0:T(1024)S(1)}, f32[256,2560]{1,0:T(8,128)S(1)}) fusion(bf16[256,2560]{1,0:T(8,128)(2,1)S(1)} %bitcast.151, bf16[3,2560]{1,0:T(4,128)(2,1)S(1)} %collective-permute-done, bf16[1,256,2560]{2,1,0:T(8,128)(2,1)S(1)} %copy-done.1, ...), kind=kLoop, calls=%fused_computation.33 | loop fusion | flops 31447040 | bytes 9282560 | tf_op jit(solution)/shard_map/reduce_sum | solution.py:61
  140.1 4.6 %collective-permute-done.2 = f32[3,2560]{1,0:T(4,128)S(1)} collective-permute-done((f32[3,2560]{1,0:T(4,128)S(1)}, f32[3,2560]{1,0:T(4,128)S(1)}, u32[]{:S(2)}, u32[]{:S(2)}) %collective-permute-start.2) | collective-permute-done | bytes 30752 | tf_op jit(solution)/shard_map/ppermute | solution.py:16
  144.7 4.6 %fusion.18 = (f32[2560]{0:T(1024)S(1)}, f32[256,2560]{1,0:T(8,128)}, bf16[1,256,2560]{2,1,0:T(8,128)(2,1)}) fusion(bf16[1,256,2560]{2,1,0:T(8,128)(2,1)S(1)} %copy-done.6, bf16[256,2560]{1,0:T(8,128)(2,1)S(1)} %bitcast.152, f32[2560]{0:T(1024)S(1)} %get-tuple-element.203, bf16[3,2560]{1,0:T(4,128)(2,1)S(1)} %collective-permute-done, ...), kind=kLoop, calls=%fused_computation.41 | loop fusion | flops 26211840 | bytes 9272320 | tf_op jit(solution)/shard_map/reduce_sum | solution.py:217
  149.3 3.2 copy.92
  152.5 2.1 multiply_convert_fusion.3
  155.7 1.9 fusion.33
  157.9 2.9 fusion.47
  162.2 2.4 fusion.55
  165.5 3.8 %fusion.48 = f32[256,128]{1,0:T(8,128)S(1)} fusion(bf16[256,40,64]{0,2,1:T(8,128)(2,1)} %copy-done.4, f32[256,40]{0,1:T(8,128)S(1)} %get-tuple-element.240), kind=kOutput, calls=%fused_computation.81 | convolution fusion | flops 504627200 | bytes 1482752 | tf_op jit(solution)/shard_map/while/body/eval_jaxpr/jhp,hpn->jn/dot_general | solution.py:151
  169.3 2.2 fusion.46
  171.5 4.5 %fusion = f32[256,256]{0,1:T(8,128)S(1)} fusion(f32[40,256]{1,0:T(8,128)S(1)} %get-tuple-element.233, pred[256,256]{0,1:T(8,128)(4,1)S(1)} %copy-done.13, bf16[256,40,64]{0,2,1:T(8,128)(2,1)S(1)} %copy-done.5, bf16[256,40,64]{0,2,1:T(8,128)(2,1)S(1)} %bitcast.156), kind=kOutput, calls=%fused_computation.5 | convolution fusion | flops 351207424 | bytes 2990080 | tf_op jit(solution)/shard_map/while/body/eval_jaxpr/ihp,jhp->hij/dot_general | solution.py:145
  176.3 77.7 %all-gather.6.cloned.1.call-done = f32[160,64,128]{2,1,0:T(8,128)} async-done(((f32[40,64,128]{2,1,0:T(8,128)}), f32[160,64,128]{2,1,0:T(8,128)}) %all-gather.6.cloned.1.call-update) | async-done | bytes 5242896 | tf_op jit(solution)/shard_map/all_gather | solution.py:23
  254.4 2.4 fusion.74
  256.8 2.2 fusion.45
  260.1 6.5 %fusion.31 = f32[256,40,64]{0,2,1:T(8,128)} fusion(f32[256,40,64]{0,2,1:T(8,128)} %fusion.74, f32[256,40,64]{0,2,1:T(8,128)} %fusion.55, bf16[256,40,64]{0,2,1:T(8,128)(2,1)} %copy-done.4, f32[256,256]{0,1:T(8,128)} %copy-done.8, f32[40,256]{1,0:T(8,128)S(1)} %get-tuple-element.233, pred[256,256]{0,1:T(8,128)(4,1)} %copy-done.12, ...), kind=kOutput, calls=%fused_computation.57 | convolution fusion | flops 351928320 | bytes 9625600 | tf_op jit(solution)/shard_map/while/body/eval_jaxpr/hij,jhp->ihp/dot_general | solution.py:116
  266.6 3.4 %copy.100 = f32[256,2560]{1,0:T(8,128)} copy(f32[256,2560]{0,1:T(8,128)} %bitcast.162) | data formatting | bytes 5242880 | tf_op jit(solution)/shard_map/reshape | solution.py:181
  270.1 3.3 %fusion.37 = bf16[1,256,2560]{2,1,0:T(8,128)(2,1)} fusion(f32[256,2560]{1,0:T(8,128)} %copy.100, f32[256,2560]{1,0:T(8,128)S(1)} %copy-done, f32[2560]{0:T(1024)S(1)} %mul.481), kind=kLoop, calls=%fused_computation.69 | loop fusion | flops 1966080 | bytes 6563840 | tf_op jit(solution)/shard_map/broadcast_in_dim | solution.py:223
  273.4 3.7 %reduce-scatter.2.cloned.1.call-done = f32[128,256]{0,1:T(8,128)} async-done(((f32[256,256]{0,1:T(8,128)}), f32[128,256]{0,1:T(8,128)}) %reduce-scatter.2.cloned.1.call-update) | async-done | bytes 131088 | tf_op jit(solution)/shard_map/reduce_scatter | solution.py:201
  278.1 4.3 %all_gather.33 = f32[4,256]{1,0:T(4,128)S(1)} all-gather(f32[4,128]{1,0:T(4,128)S(1)} %pad_maximum_fusion.4), channel_id=1, replica_groups=mesh['groups'=2,'seq'=4,'head'=2,'dp'=2] {'head'}, dimensions={1}, use_global_device_ids=true | all-gather | bytes 6144 | tf_op jit(solution)/shard_map/all_gather | solution.py:216
  282.5 28.4 %all-reduce.1 = (f32[4,2560]{1,0:T(4,128)S(1)}, f32[4,256]{1,0:T(4,128)S(1)}, f32[40]{0:T(128)S(1)}) all-reduce(f32[4,2560]{1,0:T(4,128)S(1)} %copy-done.9, f32[4,256]{1,0:T(4,128)S(1)} %all_gather.33, f32[40]{0:T(128)S(1)} %reduce_sum.119), channel_id=1, replica_groups=mesh['groups'=2,'seq'=4,'head'=2,'dp'=2] {'seq','dp'}, use_global_device_ids=true, to_apply=%region_15.16 | all-reduce | flops 11304 | bytes 90432 | tf_op jit(solution)/shard_map/psum | solution.py:218
  313.9 3.7 %collective-permute-done.3 = f32[3,128]{1,0:T(4,128)S(1)} collective-permute-done((f32[3,128]{1,0:T(4,128)S(1)}, f32[3,128]{1,0:T(4,128)S(1)}, u32[]{:S(2)}, u32[]{:S(2)}) %collective-permute-start.3) | collective-permute-done | bytes 1568 | tf_op jit(solution)/shard_map/ppermute | solution.py:16
  317.7 5.0 %all_gather.32 = bf16[256,256]{1,0:T(8,128)(2,1)S(1)} all-gather(bf16[256,128]{1,0:T(8,128)(2,1)S(1)} %fusion.62), channel_id=1, replica_groups=mesh['groups'=2,'seq'=4,'head'=2,'dp'=2] {'head'}, dimensions={1}, use_global_device_ids=true | all-gather | bytes 196608 | tf_op jit(solution)/shard_map/all_gather | solution.py:215
  (127 shorter events, 28.5 us)
Async XLA Ops:
  7.2 10.5 %copy-start.7 = (bf16[1,256,256]{2,1,0:T(8,128)(2,1)S(1)}, bf16[1,256,256]{2,1,0:T(8,128)(2,1)}, u32[]{:S(2)}) copy-start(bf16[1,256,256]{2,1,0:T(8,128)(2,1)} %param.12) | copy-start | bytes 393220
  7.2 111.1 %all-gather.8.cloned.1.call-start = ((), (), s32[]{:S(2)}) async-start(), calls=%async_computation.3 | async-start | bytes 6553600 | tf_op jit(solution)/shard_map/all_gather | solution.py:23
  7.9 9.7 %collective-permute-start.1 = (bf16[3,256]{1,0:T(4,128)(2,1)S(1)}, bf16[3,256]{1,0:T(4,128)(2,1)S(1)}, u32[]{:S(2)}, u32[]{:S(2)}) collective-permute-start(bf16[3,256]{1,0:T(4,128)(2,1)S(1)} %slice_bitcast_fusion.1), channel_id=1, source_target_pairs={{0,4},{4,8},{8,12},{1,5},{5,9},{9,13},{2,6},{6,10},{10,14},{3,7},{... | collective-permute-start | bytes 4616 | tf_op jit(solution)/shard_map/ppermute | solution.py:16
  15.9 3.8 %copy-start.16 = (f32[40]{0:T(128)}, f32[40]{0:T(128)S(1)}, u32[]{:S(2)}) copy-start(f32[40]{0:T(128)S(1)} %exponential_multiply_fusion) | copy-start | bytes 484
  17.5 23.4 %copy-start.2 = (bf16[1,256,2560]{1,2,0:T(8,128)(2,1)}, bf16[1,256,2560]{1,2,0:T(8,128)(2,1)S(1)}, u32[]{:S(2)}) copy-start(bf16[1,256,2560]{1,2,0:T(8,128)(2,1)S(1)} %copy.101) | copy-start | bytes 3932164
  17.6 2.3 copy-start.1
  17.6 5.8 %copy-start.23 = (u32[32]{0:T(128)S(1)}, u32[32]{0:T(128)}, u32[]{:S(2)}) copy-start(u32[32]{0:T(128)} %constant.137) | copy-start | bytes 388
  17.6 18.8 %copy-start.22 = (f32[40]{0:T(128)S(1)}, f32[40]{0:T(128)}, u32[]{:S(2)}) copy-start(f32[40]{0:T(128)} %param.16) | copy-start | bytes 484
  17.6 19.3 %copy-start.14 = (f32[4,2560]{1,0:T(4,128)S(1)}, f32[4,2560]{1,0:T(4,128)}, u32[]{:S(2)}) copy-start(f32[4,2560]{1,0:T(4,128)} %param.14) | copy-start | bytes 122884
  19.8 234.3 %all-gather.6.cloned.1.call-start = ((), (), s32[]{:S(2)}) async-start(), calls=%async_computation.2 | async-start | bytes 6553600 | tf_op jit(solution)/shard_map/all_gather | solution.py:23
  19.8 113.8 %collective-permute-start = (bf16[3,2560]{1,0:T(4,128)(2,1)S(1)}, bf16[3,2560]{1,0:T(4,128)(2,1)S(1)}, u32[]{:S(2)}, u32[]{:S(2)}) collective-permute-start(bf16[3,2560]{1,0:T(4,128)(2,1)S(1)} %slice_bitcast_fusion), channel_id=1, source_target_pairs={{0,4},{4,8},{8,12},{1,5},{5,9},{9,13},{2,6},{6,10},{10,14},{3,7},{... | collective-permute-start | bytes 46088 | tf_op jit(solution)/shard_map/ppermute | solution.py:16
  36.9 4.1 %copy-start.12 = (pred[256,256]{0,1:T(8,128)(4,1)}, pred[256,256]{0,1:T(8,128)(4,1)S(1)}, u32[]{:S(2)}) copy-start(pred[256,256]{0,1:T(8,128)(4,1)S(1)} %iota_compare_fusion) | copy-start | bytes 196612
  38.5 2.4 copy-start.8
  133.7 11.0 %copy-start.6 = (bf16[1,256,2560]{2,1,0:T(8,128)(2,1)S(1)}, bf16[1,256,2560]{2,1,0:T(8,128)(2,1)}, u32[]{:S(2)}) copy-start(bf16[1,256,2560]{2,1,0:T(8,128)(2,1)} %param.17) | copy-start | bytes 3932164
  138.8 5.9 %collective-permute-start.2 = (f32[3,2560]{1,0:T(4,128)S(1)}, f32[3,2560]{1,0:T(4,128)S(1)}, u32[]{:S(2)}, u32[]{:S(2)}) collective-permute-start(f32[3,2560]{1,0:T(4,128)S(1)} %slice.196), channel_id=1, source_target_pairs={{4,0},{8,4},{12,8},{5,1},{9,5},{13,9},{6,2},{10,6},{14,10},{7,3},{... | collective-permute-start | bytes 92168 | tf_op jit(solution)/shard_map/ppermute | solution.py:16
  152.5 3.2 copy-start.17
  154.6 1.1 copy-start.4
  155.7 2.2 copy-start.15
  155.7 2.2 copy-start.3
  157.6 119.4 %reduce-scatter.2.cloned.1.call-start = ((), (), s32[]{:S(2)}) async-start(), calls=%async_computation.1 | async-start | bytes 393216 | tf_op jit(solution)/shard_map/reduce_scatter | solution.py:201
  165.5 3.8 %copy-start.5 = (bf16[256,40,64]{0,2,1:T(8,128)(2,1)S(1)}, bf16[256,40,64]{0,2,1:T(8,128)(2,1)}, u32[]{:S(2)}) copy-start(bf16[256,40,64]{0,2,1:T(8,128)(2,1)} %copy-done.4) | copy-start | bytes 3932164
  165.5 6.0 %copy-start.13 = (pred[256,256]{0,1:T(8,128)(4,1)S(1)}, pred[256,256]{0,1:T(8,128)(4,1)}, u32[]{:S(2)}) copy-start(pred[256,256]{0,1:T(8,128)(4,1)} %copy-done.12) | copy-start | bytes 196612
  254.4 2.4 copy-start.10
  254.4 4.6 %copy-start.11 = (f32[256,128]{1,0:T(8,128)S(1)}, f32[256,128]{1,0:T(8,128)}, u32[]{:S(2)}) copy-start(f32[256,128]{1,0:T(8,128)} %fusion.47) | copy-start | bytes 393220
  266.6 3.4 %copy-start = (f32[256,2560]{1,0:T(8,128)S(1)}, f32[256,2560]{1,0:T(8,128)}, u32[]{:S(2)}) copy-start(f32[256,2560]{1,0:T(8,128)} %get-tuple-element.229) | copy-start | bytes 7864324
  270.0 12.5 %copy-start.9 = (f32[4,2560]{1,0:T(4,128)S(1)}, f32[4,2560]{1,0:T(4,128)}, u32[]{:S(2)}) copy-start(f32[4,2560]{1,0:T(4,128)} %pad_maximum_fusion.3) | copy-start | bytes 122884
  270.0 47.6 %copy-start.18 = (f32[128]{0:T(128)S(1)}, f32[128]{0:T(128)}, u32[]{:S(2)}) copy-start(f32[128]{0:T(128)} %get-tuple-element.248) | copy-start | bytes 1540
  270.0 47.6 %copy-start.19 = (f32[128]{0:T(128)S(1)}, f32[128]{0:T(128)}, u32[]{:S(2)}) copy-start(f32[128]{0:T(128)} %get-tuple-element.249) | copy-start | bytes 1540
  270.0 47.6 %copy-start.20 = (f32[128]{0:T(128)S(1)}, f32[128]{0:T(128)}, u32[]{:S(2)}) copy-start(f32[128]{0:T(128)} %get-tuple-element.250) | copy-start | bytes 1540
  270.1 47.6 %copy-start.21 = (f32[128]{0:T(128)S(1)}, f32[128]{0:T(128)}, u32[]{:S(2)}) copy-start(f32[128]{0:T(128)} %get-tuple-element.251) | copy-start | bytes 1540
  312.1 5.5 %collective-permute-start.3 = (f32[3,128]{1,0:T(4,128)S(1)}, f32[3,128]{1,0:T(4,128)S(1)}, u32[]{:S(2)}, u32[]{:S(2)}) collective-permute-start(f32[3,128]{1,0:T(4,128)S(1)} %slice.201), channel_id=1, source_target_pairs={{4,0},{8,4},{12,8},{5,1},{9,5},{13,9},{6,2},{10,6},{14,10},{7,3},{... | collective-permute-start | bytes 4616 | tf_op jit(solution)/shard_map/ppermute | solution.py:16
Sparse Core Ops, SparseCore 0:
  19.9 98.3 all-gather.7
  157.8 96.1 all-gather.5
  260.3 16.7 reduce-scatter.1
where the time goes:
time: 331 us; the launch traced here: 330 us
  waiting for transfers between devices  162 us (49%)
  blocking collectives  47.8 us (14%)
  matrix products  43.6 us (13%)
  other arithmetic  28.8 us (9%)
  local copies, waits for them, and re-layouts  20.7 us (6%)
  between operations  15 us (5%)
  starting transfers between devices  11.3 us (3%)
    all_gather x2, waiting for transfers between devices, carried_in(): gathered = jax.tree.map(lambda a: lax.all_gather(a, axis), part)  150 us
    psum x1, blocking collectives, local(): lax.psum((taps_x, taps_bc, skip_term), ('seq', 'dp'))  28.4 us
    ppermute x4, starting transfers between devices, shifted(): return lax.ppermute(block, axis, route)  11 us
    unnamed x1, blocking collectives  10.1 us
    ppermute x4, waiting for transfers between devices, shifted(): return lax.ppermute(block, axis, route)  8.27 us
  transfers between devices with their start and end apart: 7, of which 5 were waited for; matrix products, arithmetic and copies ran while one was open for 19% of the time, Pallas kernels for 0%

commit v1 on v0

v1 whole, which is shorter than its diff:
```python
import functools

import jax
import jax.numpy as jnp
from jax import lax
from jax.experimental import pallas as pl
from jax.experimental.pallas import tpu as pltpu
from jax.sharding import PartitionSpec as P

MESH = pl.DeviceIdType.MESH
f32 = jnp.float32
bf16 = jnp.bfloat16


def dot(a, b, ca, cb):
    return lax.dot_general(a, b, (((ca,), (cb,)), ((), ())), preferred_element_type=f32)


def expander(width, columns, head_dim):
    rows = lax.broadcasted_iota(jnp.int32, (2 * width, columns), 0) % width
    cols = lax.broadcasted_iota(jnp.int32, (2 * width, columns), 1) // head_dim
    return (rows == cols).astype(f32).astype(bf16)


def conv_taps(pad_ref, weight, first, tokens):
    total = weight[0:1, :] * pad_ref[pl.ds(first, tokens), :]
    for k in range(1, weight.shape[0]):
        total = total + weight[k : k + 1, :] * pad_ref[pl.ds(first + k, tokens), :]
    return total


def silu_parts(pre):
    sigma = jax.nn.sigmoid(pre)
    return pre * sigma, sigma * (1.0 + pre * (1.0 - sigma))


def state_kernel(
    head_dim, x_ref, halo_ref, bc_ref, bc_halo_ref, cw_ref, cbc_ref, fac_ref, g_ref,
    w_ref, inner_ref, ds_ref, s_ref, u_ref, mapped_ref, dsbc_ref, xp, bp,
):
    tokens, columns = x_ref.shape
    width = columns // head_dim
    n = mapped_ref.shape[1] // 2

    @pl.when(pl.program_id(0) == 0)
    def _():
        bp[0:8, :] = bc_halo_ref[...].astype(f32)
        bp[8 : 8 + tokens, :] = bc_ref[...].astype(f32)
        value, slope = silu_parts(conv_taps(bp, cbc_ref[...], 9 - cbc_ref.shape[0], tokens))
        mapped_ref[...] = value.astype(bf16)
        dsbc_ref[...] = slope

    xp[0:8, :] = halo_ref[...].astype(f32)
    xp[8 : 8 + tokens, :] = x_ref[...].astype(f32)
    value, slope = silu_parts(conv_taps(xp, cw_ref[...], 9 - cw_ref.shape[0], tokens))
    inner = value.astype(bf16)
    inner_ref[...] = inner
    ds_ref[...] = slope.astype(bf16)
    spread = dot(fac_ref[0], expander(width, columns, head_dim), 1, 0)
    w = (inner.astype(f32) * spread[:tokens]).astype(bf16)
    w_ref[...] = w
    lead = (g_ref[...].astype(f32) * spread[tokens : 2 * tokens]).astype(bf16)
    tail = (w.astype(f32) * spread[2 * tokens :]).astype(bf16)
    s_ref[0] = dot(mapped_ref[:, :n], tail, 0, 0).astype(bf16)
    u_ref[0] = dot(mapped_ref[:, n:], lead, 0, 0).astype(bf16)


def carry_kernel(
    devices, s_ref, u_ref, et_ref, p_ref, q_ref, out_f, out_b, send_f, recv_f, send_b, recv_b
):
    me = lax.axis_index("seq")
    chunks = s_ref.shape[0]
    barrier = pltpu.get_barrier_semaphore()
    for other in (lax.rem(me + 1, devices), lax.rem(me + devices - 1, devices)):
        pl.semaphore_signal(barrier, inc=1, device_id={"seq": other}, device_id_type=MESH)
    pl.semaphore_wait(barrier, 2)

    def forward(c):
        return pltpu.make_async_remote_copy(
            src_ref=out_f.at[c], dst_ref=p_ref.at[c], send_sem=send_f.at[c],
            recv_sem=recv_f.at[c], device_id={"seq": me + 1}, device_id_type=MESH,
        )

    def backward(c):
        return pltpu.make_async_remote_copy(
            src_ref=out_b.at[c], dst_ref=q_ref.at[c], send_sem=send_b.at[c],
            recv_sem=recv_b.at[c], device_id={"seq": me - 1}, device_id_type=MESH,
        )

    def advance(c, place, make, own_ref, in_ref, out_ref):
        @pl.when(place == 0)
        def _():
            in_ref[c] = jnp.zeros(in_ref.shape[1:], in_ref.dtype)
            out_ref[c] = own_ref[c]

        @pl.when(place > 0)
        def _():
            make(c).wait_recv()
            out_ref[c] = (in_ref[c].astype(f32) * et_ref[c] + own_ref[c].astype(f32)).astype(bf16)

        @pl.when(place < devices - 1)
        def _():
            make(c).start()

    back = devices - 1 - me

    @pl.loop(0, chunks + devices - 1)
    def _(step):
        cf = step - me
        cb = step - back

        @pl.when((cf >= 0) & (cf < chunks))
        def _():
            advance(cf, me, forward, s_ref, p_ref, out_f)

        @pl.when((cb >= 0) & (cb < chunks))
        def _():
            advance(cb, back, backward, u_ref, q_ref, out_b)

    @pl.loop(0, chunks)
    def _(c):
        @pl.when(me < devices - 1)
        def _():
            forward(c).wait_send()

        @pl.when(me > 0)
        def _():
            backward(c).wait_send()


def apply_kernel(
    head_dim, scale, x_ref, halo_ref, cw_ref, fac_ref, ct_ref, cr_ref, skip_ref, g_ref, w_ref,
    inner_ref, ds_ref, mapped_ref, dsbc_ref, p_ref, q_ref,
    y_ref, gx_ref, edge_ref, taps_ref, dbc_ref, sim, dsim, dbc, xp, dp, ya, da,
):
    tokens, columns = x_ref.shape
    width = columns // head_dim
    n = mapped_ref.shape[1] // 2
    taps = cw_ref.shape[0]
    lower = lax.broadcasted_iota(jnp.int32, (tokens, tokens), 0) >= lax.broadcasted_iota(
        jnp.int32, (tokens, tokens), 1
    )
    b_mat = mapped_ref[:, :n]
    c_mat = mapped_ref[:, n:]

    @pl.when(pl.program_id(0) == 0)
    def _():
        sim[...] = dot(c_mat, b_mat, 1, 1)
        dsim[...] = jnp.zeros_like(dsim)
        dbc[...] = jnp.zeros_like(dbc)

    pair = 2 * head_dim
    side = lax.broadcasted_iota(jnp.int32, (1, pair), 1) < head_dim
    for j in range(width // 2):
        cols = slice(j * pair, (j + 1) * pair)
        w_pair = w_ref[:, cols]
        g_pair = g_ref[:, cols]
        parts = []
        for e in range(2):
            h = 2 * j + e
            diff = ct_ref[0, :, h : h + 1] - cr_ref[0, h : h + 1, :]
            decay = jnp.exp(jnp.where(lower, diff, -1e30))
            mix = (decay * sim[...]).astype(bf16)
            mine = side if e == 0 else jnp.logical_not(side)
            g_own = jnp.where(mine, g_pair.astype(f32), 0.0).astype(bf16)
            dsim[...] += decay * dot(g_own, w_pair, 1, 1)
            parts.append((dot(mix, w_pair, 1, 0), dot(mix, g_pair, 0, 0)))
        ya[:, cols] = jnp.where(side, parts[0][0], parts[1][0])
        da[:, cols] = jnp.where(side, parts[0][1], parts[1][1])

    spread = dot(fac_ref[0], expander(width, columns, head_dim), 1, 0)
    gain = spread[:tokens]
    lead = spread[tokens : 2 * tokens]
    tail = spread[2 * tokens :]
    g = g_ref[...].astype(f32)
    inner = inner_ref[...].astype(f32)
    p = p_ref[0]
    q = q_ref[0]
    y = scale * (ya[...] + lead * dot(c_mat, p, 1, 0)) + skip_ref[...] * inner
    y_ref[...] = y.astype(bf16)
    d_w = scale * (da[...] + tail * dot(b_mat, q, 1, 0))
    d_pre = (gain * d_w + skip_ref[...] * g) * ds_ref[...].astype(f32)
    dbc[:, :n] += dot((w_ref[...].astype(f32) * tail).astype(bf16), q, 1, 1)
    dbc[:, n:] += dot((g * lead).astype(bf16), p, 1, 1)

    xp[0:8, :] = halo_ref[...].astype(f32)
    xp[8 : 8 + tokens, :] = x_ref[...].astype(f32)
    dp[0:tokens, :] = d_pre
    dp[tokens : tokens + 8, :] = jnp.zeros((8, columns), f32)
    total = jnp.zeros((tokens, columns), f32)
    for k in range(taps):
        total = total + cw_ref[k : k + 1, :] * dp[pl.ds(taps - 1 - k, tokens), :]
        taps_ref[k : k + 1, :] = jnp.sum(
            d_pre * xp[pl.ds(9 - taps + k, tokens), :], axis=0, keepdims=True
        )
    gx_ref[...] = total.astype(bf16)
    taps_ref[taps : taps + 1, :] = jnp.sum(g * inner, axis=0, keepdims=True)
    taps_ref[taps + 1 :, :] = jnp.zeros((8 - taps - 1, columns), f32)
    edge_ref[...] = d_pre[0:8]

    @pl.when(pl.program_id(0) == pl.num_programs(0) - 1)
    def _():
        d_sim = dsim[...].astype(bf16)
        d_b = dbc[:, :n] + dot(d_sim, c_mat, 0, 0)
        d_c = dbc[:, n:] + dot(d_sim, b_mat, 1, 0)
        dbc_ref[:, :n] = scale * d_b * dsbc_ref[:, :n]
        dbc_ref[:, n:] = scale * d_c * dsbc_ref[:, n:]


def shifted(block, axis, distance):
    devices = range(lax.axis_size(axis))
    route = [(i - distance, i) for i in devices if i - distance in devices]
    return lax.ppermute(block, axis, route)


def local(x_input, bc_input, decays, conv_x, conv_bc, skip_gain, grad_out):
    x = x_input[0]
    bc = bc_input[0]
    d = decays[0]
    g = grad_out[0]
    tokens, channels = x.shape
    taps = conv_x.shape[0]
    heads = d.shape[0]
    head_dim = channels // heads
    n = bc.shape[1] // 2
    scale = float(n) ** (-0.5)
    seq = lax.axis_size("seq")
    width = next(k for k in (8, 4, 2) if heads % k == 0)
    groups = heads // width
    columns = width * head_dim

    halo = shifted(jnp.concatenate([x[tokens - 8 :], bc[tokens - 8 :]], axis=1), "seq", 1)
    halo_x = halo[:, :channels]
    halo_bc = halo[:, channels:]

    cum = jnp.cumsum(jnp.log(d), axis=1)
    total = cum[:, -1:]
    factors = jnp.stack([jnp.sqrt((1.0 - d) * (1.0 + d)), jnp.exp(cum), jnp.exp(total - cum)])
    factors = factors.reshape(3, groups, width, tokens).transpose(1, 0, 3, 2)
    factors = factors.reshape(groups, 3 * tokens, width)
    high = lax.reduce_precision(factors, 8, 7)
    fac = jnp.concatenate([high.astype(bf16), (factors - high).astype(bf16)], axis=2)
    cum_r = cum.reshape(groups, width, tokens)
    cum_t = cum_r.transpose(0, 2, 1)
    et = jnp.repeat(jnp.exp(total[:, 0]), head_dim).reshape(groups, 1, columns)
    skip = jnp.repeat(skip_gain, head_dim)[None, :]

    def cols(rows):
        return pl.BlockSpec((rows, columns), lambda i: (0, i))

    def whole(rows, c):
        return pl.BlockSpec((rows, c), lambda i: (0, 0))

    def chunk(a, b):
        return pl.BlockSpec((1, a, b), lambda i: (i, 0, 0))

    def out(shape, dtype):
        return jax.ShapeDtypeStruct(shape, dtype)

    params = pltpu.CompilerParams(
        dimension_semantics=("arbitrary",), vmem_limit_bytes=48 * 1024 * 1024
    )
    w, inner, slope, s_own, u_own, mapped, slope_bc = pl.pallas_call(
        functools.partial(state_kernel, head_dim),
        grid=(groups,),
        in_specs=[
            cols(tokens), cols(8), whole(tokens, 2 * n), whole(8, 2 * n), cols(taps),
            whole(taps, 2 * n), chunk(3 * tokens, 2 * width), cols(tokens),
        ],
        out_specs=[
            cols(tokens), cols(tokens), cols(tokens), chunk(n, columns), chunk(n, columns),
            whole(tokens, 2 * n), whole(tokens, 2 * n),
        ],
        out_shape=[
            out((tokens, channels), bf16), out((tokens, channels), bf16),
            out((tokens, channels), bf16), out((groups, n, columns), bf16),
            out((groups, n, columns), bf16), out((tokens, 2 * n), bf16), out((tokens, 2 * n), f32),
        ],
        scratch_shapes=[
            pltpu.VMEM((tokens + 8, columns), f32), pltpu.VMEM((tokens + 8, 2 * n), f32),
        ],
        compiler_params=params,
        name="states",
    )(x, halo_x, bc, halo_bc, conv_x, conv_bc, fac, g)

    vmem = pl.BlockSpec(memory_space=pltpu.VMEM)
    p_in, q_in = pl.pallas_call(
        functools.partial(carry_kernel, seq),
        in_specs=[vmem] * 3,
        out_specs=[vmem] * 2,
        out_shape=[out((groups, n, columns), bf16)] * 2,
        scratch_shapes=[pltpu.VMEM((groups, n, columns), bf16)] * 2
        + [pltpu.SemaphoreType.DMA((groups,))] * 4,
        compiler_params=pltpu.CompilerParams(
            collective_id=0, has_side_effects=True, vmem_limit_bytes=32 * 1024 * 1024
        ),
        name="carry",
    )(s_own, u_own, et)

    y, gx, edge, taps_part, d_bc = pl.pallas_call(
        functools.partial(apply_kernel, head_dim, scale),
        grid=(groups,),
        in_specs=[
            cols(tokens), cols(8), cols(taps), chunk(3 * tokens, 2 * width),
            chunk(tokens, width), chunk(width, tokens), cols(1), cols(tokens), cols(tokens),
            cols(tokens), cols(tokens), whole(tokens, 2 * n), whole(tokens, 2 * n),
            chunk(n, columns), chunk(n, columns),
        ],
        out_specs=[cols(tokens), cols(tokens), cols(8), cols(8), whole(tokens, 2 * n)],
        out_shape=[
            out((tokens, channels), bf16), out((tokens, channels), bf16), out((8, channels), f32),
            out((8, channels), f32), out((tokens, 2 * n), f32),
        ],
        scratch_shapes=[
            pltpu.VMEM((tokens, tokens), f32), pltpu.VMEM((tokens, tokens), f32),
            pltpu.VMEM((tokens, 2 * n), f32), pltpu.VMEM((tokens + 8, columns), f32),
            pltpu.VMEM((tokens + 8, columns), f32), pltpu.VMEM((tokens, columns), f32),
            pltpu.VMEM((tokens, columns), f32),
        ],
        compiler_params=params,
        name="apply",
    )(
        x, halo_x, conv_x, fac, cum_t, cum_r, skip, g, w, inner, slope, mapped, slope_bc, p_in, q_in
    )

    d_bc = lax.psum(d_bc, "head")
    next_rows = shifted(jnp.concatenate([edge, d_bc[:8]], axis=1), "seq", -1)

    def fix(rows_out, next_part, weight):
        last = []
        for r in range(taps - 1):
            row = jnp.zeros((1, weight.shape[1]), f32)
            for k in range(r + 1):
                row = row + weight[k : k + 1] * next_part[r - k : r - k + 1]
            last.append(row)
        return jnp.concatenate(last, axis=0)

    fix_x = fix(gx, next_rows[:, :channels], conv_x)
    gx = gx.at[tokens - taps + 1 :].add(fix_x.astype(bf16))
    dpad = jnp.concatenate([d_bc, next_rows[: taps - 1, channels:]], axis=0)
    bpad = jnp.concatenate([halo_bc[8 - taps + 1 :], bc], axis=0).astype(f32)
    gbc = sum(conv_bc[k][None] * dpad[taps - 1 - k : taps - 1 - k + tokens] for k in range(taps))
    taps_bc = jnp.stack([jnp.sum(d_bc * bpad[k : k + tokens], axis=0) for k in range(taps)])
    taps_bc = jnp.pad(taps_bc, ((0, 8 - taps), (0, 0)))
    sums = lax.psum(jnp.concatenate([taps_part, taps_bc], axis=1), ("seq", "dp"))
    token_count = tokens * seq * lax.axis_size("dp")
    norm_tokens = float(token_count) ** (-0.5)
    norm_skip = float(token_count * head_dim) ** (-0.5)
    skip_sum = jnp.sum(sums[taps, :channels].reshape(heads, head_dim), axis=1)
    return (
        y[None],
        gx[None],
        gbc.astype(bf16)[None],
        sums[:taps, :channels] * norm_tokens,
        sums[:taps, channels:] * norm_tokens,
        skip_sum * norm_skip,
    )


def solution(mesh):
    return jax.shard_map(
        local,
        mesh=mesh,
        in_specs=(
            P(("groups", "dp"), "seq", "head"),
            P(("groups", "dp"), "seq", None),
            P(("groups", "dp"), "head", "seq"),
            P(None, "head"),
            P(),
            P("head"),
            P(("groups", "dp"), "seq", "head"),
        ),
        out_specs=(
            P(("groups", "dp"), "seq", "head"),
            P(("groups", "dp"), "seq", "head"),
            P(("groups", "dp"), "seq", None),
            P("groups", "head"),
            P("groups", None),
            P(("groups", "head")),
        ),
        check_vma=False,
    )
```

time: 331 us -> 172 us (0.52)
  waiting for transfers between devices: 162 us -> 74.5 us
  Pallas kernels: 0 us -> 58.2 us
  blocking collectives: 47.8 us -> 0 us
  matrix products: 43.6 us -> 0 us
  other arithmetic: 28.8 us -> 9 us
  local copies, waits for them, and re-layouts: 20.7 us -> 8.38 us
  starting transfers between devices: 11.3 us -> 6.28 us
    all_gather x2 -> x0, waiting for transfers between devices: 150 us -> none  [carried_in(): gathered = jax.tree.map(lambda a: lax.all_gather(a, axis), part)]
    psum x0 -> x2, waiting for transfers between devices: none -> 69.3 us  [the longest x1 47.9 us: local(): lax.psum(jnp.concatenate([taps_part, taps_bc], axis=1), ('seq', 'dp'))]
    pallas_call x0 -> x3, Pallas kernels: none -> 58.2 us  [the longest x1 33.5 us: local(): pl.pallas_call(functools.partial(carry_kernel, seq), in_specs=[vmem] * 3,...]
    dot_general x16 -> x0, matrix products: 43.6 us -> none  [the longest x1 6.48 us: forward_block(): jnp.einsum('hij,jhp->ihp', mixing, w_b, preferred_element_type=jnp.float32)]
    psum x1 -> x0, blocking collectives: 28.4 us -> none  [local(): lax.psum((taps_x, taps_bc, skip_term), ('seq', 'dp'))]
    unnamed x1 -> x0, blocking collectives: 10.1 us -> none
    all_gather x2 -> x0, blocking collectives: 9.3 us -> none  [the longest x1 4.96 us: local(): grad_bc_rows = lax.all_gather(grad_bc_part, 'head', axis=1, tiled=True)]
    reduce_sum x4 -> x2, other arithmetic: 10.9 us -> 2.34 us  [the longest x1 2.23 us: local(): jnp.sum(d_bc * bpad[k:k + tokens], axis=0)]
  transfers between devices with their start and end apart: 7 -> 4, of which waited for: 5 -> 3; matrix products, arithmetic and copies ran while one was open for 19% -> 3% of each run, Pallas kernels for 0% -> 0%
where the time goes in v1:
time: 172 us; the launch traced here: 171 us
  waiting for transfers between devices  74.5 us (43%)
  Pallas kernels  58.2 us (34%)
  between operations  14.3 us (8%)
  other arithmetic  9 us (5%)
  local copies, waits for them, and re-layouts  8.38 us (5%)
  starting transfers between devices  6.28 us (4%)
    psum x1, waiting for transfers between devices, local(): lax.psum(jnp.concatenate([taps_part, taps_bc], axis=1), ('seq', 'dp'))  47.9 us
    pallas_call x1, Pallas kernels, local(): pl.pallas_call(functools.partial(carry_kernel, seq), in_specs=[vmem] * 3,...  33.5 us
    psum x1, waiting for transfers between devices, local(): d_bc = lax.psum(d_bc, 'head')  21.5 us
    pallas_call x1, Pallas kernels, local(): pl.pallas_call(functools.partial(apply_kernel, head_dim, scale), grid=(gr...  16.2 us
    pallas_call x1, Pallas kernels, local(): pl.pallas_call(functools.partial(state_kernel, head_dim), grid=(groups,),...  8.53 us
    ppermute x2, starting transfers between devices, shifted(): return lax.ppermute(block, axis, route)  6.2 us
    ppermute x2, waiting for transfers between devices, shifted(): return lax.ppermute(block, axis, route)  5.09 us
  transfers between devices with their start and end apart: 4, of which 3 were waited for; matrix products, arithmetic and copies ran while one was open for 3% of the time, Pallas kernels for 0%

profile of v1, /device:TPU:0, one launch (start us, length us, event | category | flops | bytes accessed | tf_op | source)
XLA Modules:
  0.0 170.7 jit_solution(13339156826408375658)
XLA Ops:
  7.2 0.8 slice_bitcast_fusion
  8.0 0.7 slice_bitcast_fusion.1
  8.7 4.9 %collective-permute-start = (bf16[8,2816]{1,0:T(8,128)(2,1)S(1)}, bf16[8,2816]{1,0:T(8,128)(2,1)S(1)}, u32[]{:S(2)}, u32[]{:S(2)}) collective-permute-start(bf16[8,2816]{1,0:T(8,128)(2,1)S(1)} %pad_maximum_fusion.4), channel_id=1, source_target_pairs={{0,4},{4,8},{8,12},{1,5},{5,9},{9,13},{2,6},{6,10},{10,14},{3,7},{... | collective-permute-start | bytes 135176 | tf_op jit(solution)/shard_map/ppermute | solution.py:213
  13.6 0.8 sqrt_bitcast_fusion
  14.5 0.6 reduce-window.6
  15.1 0.2 slice_reduce_fusion
  15.3 0.1 copy_bitcast_fusion
  15.5 0.2 slice_reduce_fusion.1
  15.8 0.1 fusion.19
  16.0 0.5 copy.42.fac_ref
  16.6 0.1 broadcast_in_dim.21.et_ref
  16.7 0.2 copy.43.ct_ref
  17.0 0.1 broadcast_in_dim_reshape.3.skip_ref
  17.2 8.5 %states.1 = (bf16[256,2560]{1,0:T(8,128)(2,1)S(1)}, bf16[256,2560]{1,0:T(8,128)(2,1)S(1)}, bf16[256,2560]{1,0:T(8,128)(2,1)}, bf16[5,128,512]{2,1,0:T(8,128)(2,1...) custom-call(bf16[256,2560]{1,0:T(8,128)(2,1)} %bitcast.32, ...), custom_call_target="tpu_custom_call" | custom-call | tf_op jit(solution)/shard_map/states/pallas_call | solution.py:263
  25.7 1.1 copy-done.1
  26.8 1.1 copy-done.2
  27.9 33.5 %carry.1 = (bf16[5,128,512]{2,1,0:T(8,128)(2,1)S(1)}, bf16[5,128,512]{2,1,0:T(8,128)(2,1)S(1)}) custom-call(bf16[5,128,512]{2,1,0:T(8,128)(2,1)S(1)} %get-tuple-element.37.s_ref, bf16[5,128,512]{2,1,0:T(8,128)(2,1)S(1)} %get-tuple-element.38.u_ref, f32[5,1,512]{2,1,0:T(1,128)S(1)} %broadcast_in_dim.21.et_ref), custom_call_target="tpu_custom_call" | custom-call | tf_op jit(solution)/shard_map/carry/pallas_call | solution.py:287
  61.4 16.2 %apply.1 = (bf16[256,2560]{1,0:T(8,128)(2,1)}, bf16[256,2560]{1,0:T(8,128)(2,1)}, f32[8,2560]{1,0:T(8,128)S(1)}, f32[8,2560]{1,0:T(8,128)S(1)}, f32[256,256]{1,0:T(8,128)}) custom-call(bf16[256,2560]{1,0:T(8,128)(2,1)S(1)} %bitcast.33, bf16[8,2560]{1,0:T(8,128)(2,1)S(1)} %slice.159.halo_ref, f32[4,2560]{1,0:T(4,128)S(1)} %copy-done.4, ...), custom_call_target="tpu_custom_call" | custom-call | tf_op jit(solution)/shard_map/apply/pallas_call | solution.py:300
  77.6 21.5 %all-reduce.4.cloned.1.call-done = f32[256,256]{1,0:T(8,128)} async-done(((f32[256,256]{1,0:T(8,128)}), f32[256,256]{1,0:T(8,128)}) %all-reduce.4.cloned.1.call-update) | async-done | bytes 262160 | tf_op jit(solution)/shard_map/psum | solution.py:326
  99.1 0.7 slice.163
  99.8 1.3 collective-permute-start.1
  101.1 5.1 %collective-permute-done.1 = f32[8,2816]{1,0:T(8,128)S(1)} collective-permute-done((f32[8,2816]{1,0:T(8,128)S(1)}, f32[8,2816]{1,0:T(8,128)S(1)}, u32[]{:S(2)}, u32[]{:S(2)}) %collective-permute-start.1) | collective-permute-done | bytes 90144 | tf_op jit(solution)/shard_map/ppermute | solution.py:213
  106.2 2.2 %fusion.11 = (f32[256]{0:T(256)S(1)}, f32[256]{0:T(256)S(1)}, f32[256]{0:T(256)S(1)}, f32[256]{0:T(256)S(1)}, bf16[1,256,256]{2,1,0:T(8,128)(2,1)}) fusion(f32[256,256]{1,0:T(8,128)} %all-reduce.4.cloned.1.call-done, f32[259,256]{1,0:T(8,128)S(1)} %maximum_convert_fusion, f32[256]{0:T(256)S(1)} %bitcast.46, f32[3,256]{1,0:T(4,128)S(1)} %slice.167, ...), kind=kLoop, calls=%fused_computation.17 | loop fusion | flops 1244160 | bytes 1453056 | tf_op jit(solution)/shard_map/reduce_sum | solution.py:343
  108.5 0.6 pad_maximum_fusion.3
  109.2 0.8 fusion.15
  110.0 1.4 scatter-add.4
  111.5 47.9 %all-reduce.6.cloned.1.call-done = f32[8,2816]{1,0:T(8,128)} async-done(((f32[8,2816]{1,0:T(8,128)}), f32[8,2816]{1,0:T(8,128)}) %all-reduce.6.cloned.1.call-update) | async-done | bytes 90128 | tf_op jit(solution)/shard_map/psum | solution.py:345
  159.4 0.9 slice_reduce_fusion.2
  160.4 0.1 reduce_sum.49
  160.5 0.5 broadcast_multiply_fusion
  161.0 1.5 slice_multiply_fusion.4
  162.5 1.3 slice_multiply_fusion.6
  (44 shorter events, 0.9 us)
Async XLA Ops:
  7.2 91.9 %all-reduce.4.cloned.1.call-start = ((), (), s32[]{:S(2)}) async-start(), calls=%async_computation | async-start | bytes 524288 | tf_op jit(solution)/shard_map/psum | solution.py:326
  8.7 8.4 %collective-permute-start = (bf16[8,2816]{1,0:T(8,128)(2,1)S(1)}, bf16[8,2816]{1,0:T(8,128)(2,1)S(1)}, u32[]{:S(2)}, u32[]{:S(2)}) collective-permute-start(bf16[8,2816]{1,0:T(8,128)(2,1)S(1)} %pad_maximum_fusion.4), channel_id=1, source_target_pairs={{0,4},{4,8},{8,12},{1,5},{5,9},{9,13},{2,6},{6,10},{10,14},{3,7},{... | collective-permute-start | bytes 135176 | tf_op jit(solution)/shard_map/ppermute | solution.py:213
  15.9 1.0 copy-start.6
  15.9 1.2 copy-start.3
  15.9 1.2 copy-start.4
  15.9 1.2 copy-start.5
  25.7 1.1 copy-start.1
  26.8 1.1 copy-start.2
  27.9 33.5 %copy-start = (bf16[1,256,2560]{2,1,0:T(8,128)(2,1)S(1)}, bf16[1,256,2560]{2,1,0:T(8,128)(2,1)}, u32[]{:S(2)}) copy-start(bf16[1,256,2560]{2,1,0:T(8,128)(2,1)} %param.9) | copy-start | bytes 3932164
  77.6 81.8 %all-reduce.6.cloned.1.call-start = ((), (), s32[]{:S(2)}) async-start(), calls=%async_computation.1 | async-start | bytes 180224 | tf_op jit(solution)/shard_map/psum | solution.py:345
  99.8 6.4 %collective-permute-start.1 = (f32[8,2816]{1,0:T(8,128)S(1)}, f32[8,2816]{1,0:T(8,128)S(1)}, u32[]{:S(2)}, u32[]{:S(2)}) collective-permute-start(f32[8,2816]{1,0:T(8,128)S(1)} %pad_maximum_fusion.2), channel_id=1, source_target_pairs={{4,0},{8,4},{12,8},{5,1},{9,5},{13,9},{6,2},{10,6},{14,10},{7,3},{... | collective-permute-start | bytes 270344 | tf_op jit(solution)/shard_map/ppermute | solution.py:213
Sparse Core Ops, SparseCore 0:
  77.7 21.3 all-reduce.3
  109.3 50.0 all-reduce.5

commit v2 on v1

--- a/solution.py
+++ b/solution.py
@@ -131,7 +131,7 @@
 def apply_kernel(
     head_dim, scale, x_ref, halo_ref, cw_ref, fac_ref, ct_ref, cr_ref, skip_ref, g_ref, w_ref,
     inner_ref, ds_ref, mapped_ref, dsbc_ref, p_ref, q_ref,
-    y_ref, gx_ref, edge_ref, taps_ref, dbc_ref, sim, dsim, dbc, xp, dp, ya, da,
+    y_ref, gx_ref, tail_ref, edge_ref, taps_ref, dbc_ref, sim, dsim, dbc, xp, dp, ya, da,
 ):
     tokens, columns = x_ref.shape
     width = columns // head_dim
@@ -194,6 +194,7 @@
             d_pre * xp[pl.ds(9 - taps + k, tokens), :], axis=0, keepdims=True
         )
     gx_ref[...] = total.astype(bf16)
+    tail_ref[...] = total[tokens - 16 :]
     taps_ref[taps : taps + 1, :] = jnp.sum(g * inner, axis=0, keepdims=True)
     taps_ref[taps + 1 :, :] = jnp.zeros((8 - taps - 1, columns), f32)
     edge_ref[...] = d_pre[0:8]
@@ -203,8 +204,190 @@
         d_sim = dsim[...].astype(bf16)
         d_b = dbc[:, :n] + dot(d_sim, c_mat, 0, 0)
         d_c = dbc[:, n:] + dot(d_sim, b_mat, 1, 0)
-        dbc_ref[:, :n] = scale * d_b * dsbc_ref[:, :n]
-        dbc_ref[:, n:] = scale * d_c * dsbc_ref[:, n:]
+        dbc_ref[:, :n] = (scale * d_b * dsbc_ref[:, :n]).astype(bf16)
+        dbc_ref[:, n:] = (scale * d_c * dsbc_ref[:, n:]).astype(bf16)
+
+
+def finish_kernel(
+    sizes, norm, tail_ref, edge_ref, taps_ref, dbc_ref, bc_ref, bc_halo_ref, cw_ref, cbc_ref,
+    gbc_ref, gx_ref, sums_ref, bsum_ref, part, rs_in, red, ag_in, bct, bct_in, head_in, next_bc,
+    next_x, bp, dp, rs_send, rs_recv, ag_send, ag_recv, bc_send, bc_recv, head_send, head_recv,
+    edge_send, edge_recv, nbc_send, nbc_recv,
+):
+    seq, heads, cores = sizes
+    members = seq * cores
+    z = lax.axis_index("seq")
+    hd = lax.axis_index("head")
+    core = lax.axis_index("dp")
+    me = z * cores + core
+    tokens = dbc_ref.shape[0]
+    taps = cw_ref.shape[0]
+    channels = taps_ref.shape[1]
+    share = part.shape[2]
+
+    def member(offset):
+        at = lax.rem(me + offset, members)
+        return at, {"seq": at // cores, "dp": lax.rem(at, cores)}
+
+    barrier = pltpu.get_barrier_semaphore()
+    targets = [member(o)[1] for o in range(1, members)]
+    for o in range(1, heads):
+        other = lax.rem(hd + o, heads)
+        targets.append({"head": other})
+        targets.append({"head": other, "seq": lax.rem(z + 1, seq)})
+        targets.append({"head": other, "seq": lax.rem(z + seq - 1, seq)})
+    for target in targets:
+        pl.semaphore_signal(barrier, inc=1, device_id=target, device_id_type=MESH)
+
+    for i in range(members):
+        low = min(i * share, channels)
+        high = min(low + share, channels)
+        if high - low < share:
+            part[i] = jnp.zeros(part.shape[1:], f32)
+        if high > low:
+            part[i, :, 0 : high - low] = taps_ref[:, low:high]
+    pl.semaphore_wait(barrier, len(targets))
+
+    def head_copy(o):
+        return pltpu.make_async_remote_copy(
+            src_ref=dbc_ref, dst_ref=head_in.at[hd], send_sem=head_send.at[o],
+            recv_sem=head_recv.at[hd], device_id={"head": lax.rem(hd + o, heads)},
+            device_id_type=MESH,
+        )
+
+    def nbc_copy(o):
+        return pltpu.make_async_remote_copy(
+            src_ref=dbc_ref.at[0:16], dst_ref=next_bc.at[hd], send_sem=nbc_send.at[o],
+            recv_sem=nbc_recv.at[hd],
+            device_id={"head": lax.rem(hd + o, heads), "seq": z - 1}, device_id_type=MESH,
+        )
+
+    def edge_copy():
+        return pltpu.make_async_remote_copy(
+            src_ref=edge_ref, dst_ref=next_x, send_sem=edge_send, recv_sem=edge_recv,
+            device_id={"seq": z - 1}, device_id_type=MESH,
+        )
+
+    def rs_copy(o):
+        at, device = member(o)
+        return pltpu.make_async_remote_copy(
+            src_ref=part.at[at], dst_ref=rs_in.at[me], send_sem=rs_send.at[o],
+            recv_sem=rs_recv.at[me], device_id=device, device_id_type=MESH,
+        )
+
+    def ag_copy(o):
+        return pltpu.make_async_remote_copy(
+            src_ref=red, dst_ref=ag_in.at[me], send_sem=ag_send.at[o],
+            recv_sem=ag_recv.at[me], device_id=member(o)[1], device_id_type=MESH,
+        )
+
+    def bct_copy(o):
+        return pltpu.make_async_remote_copy(
+            src_ref=bct, dst_ref=bct_in.at[me], send_sem=bc_send.at[o],
+            recv_sem=bc_recv.at[me], device_id=member(o)[1], device_id_type=MESH,
+        )
+
+    def arrived(slots, sem, at, source):
+        pltpu.make_async_remote_copy(
+            src_ref=source, dst_ref=slots.at[at], send_sem=sem.at[at], recv_sem=sem.at[at],
+            device_id=member(1)[1], device_id_type=MESH,
+        ).wait_recv()
+
+    for o in range(1, heads):
+        head_copy(o).start()
+    for o in range(1, members):
+        rs_copy(o).start()
+
+    @pl.when(z > 0)
+    def _():
+        for o in range(heads):
+            nbc_copy(o).start()
+        edge_copy().start()
+
+    head_in[hd] = dbc_ref[...]
+    rs_in[me] = part[me]
+    bp[0:8, :] = bc_halo_ref[...].astype(f32)
+    bp[8 : 8 + tokens, :] = bc_ref[...].astype(f32)
+
+    for o in range(1, heads):
+        arrived(head_in, head_recv, lax.rem(hd + o, heads), dbc_ref)
+    full = head_in[0].astype(f32)
+    for h in range(1, heads):
+        full = full + head_in[h].astype(f32)
+    for k in range(taps):
+        bct[k : k + 1, :] = jnp.sum(
+            full * bp[pl.ds(9 - taps + k, tokens), :], axis=0, keepdims=True
+        )
+    bct[taps:, :] = jnp.zeros((8 - taps, bct.shape[1]), f32)
+    for o in range(1, members):
+        bct_copy(o).start()
+    for o in range(1, members):
+        arrived(rs_in, rs_recv, lax.rem(me + o, members), part.at[0])
+    total = rs_in[0]
+    for i in range(1, members):
+        total = total + rs_in[i]
+    red[...] = total
+    for o in range(1, members):
+        ag_copy(o).start()
+    ag_in[me] = total
+    bct_in[me] = bct[...]
+
+    dp[0:tokens, :] = full
+    gx_ref[...] = tail_ref[...].astype(bf16)
+
+    @pl.when(z == seq - 1)
+    def _():
+        dp[tokens : tokens + 8, :] = jnp.zeros((8, full.shape[1]), f32)
+
+    @pl.when(z < seq - 1)
+    def _():
+        for o in range(heads):
+            arrived(next_bc, nbc_recv, o, dbc_ref.at[0:16])
+        edge_copy().wait_recv()
+        rows = next_bc[0].astype(f32)
+        for h in range(1, heads):
+            rows = rows + next_bc[h].astype(f32)
+        dp[tokens : tokens + 8, :] = rows[0:8]
+        at = lax.broadcasted_iota(jnp.int32, (16, 1), 0)
+        fixed = tail_ref[...]
+        for r in range(taps - 1):
+            row = jnp.zeros((1, channels), f32)
+            for k in range(r + 1):
+                row = row + cw_ref[k : k + 1, :] * next_x[r - k : r - k + 1, :]
+            fixed = fixed + jnp.where(at == 16 - (taps - 1) + r, row, 0.0)
+        gx_ref[...] = fixed.astype(bf16)
+
+    grad = jnp.zeros(full.shape, f32)
+    for k in range(taps):
+        grad = grad + cbc_ref[k : k + 1, :] * dp[pl.ds(taps - 1 - k, tokens), :]
+    gbc_ref[...] = grad.astype(bf16)
+
+    for o in range(1, members):
+        at = lax.rem(me + o, members)
+        arrived(ag_in, ag_recv, at, red)
+        arrived(bct_in, bc_recv, at, bct)
+    bsum = bct_in[0]
+    for i in range(1, members):
+        bsum = bsum + bct_in[i]
+    bsum_ref[...] = bsum[0:taps] * norm
+    for i in range(members):
+        low = min(i * share, channels)
+        high = min(low + share, channels)
+        if high > low:
+            sums_ref[:, low:high] = ag_in[i, :, 0 : high - low] * norm
+
+    for o in range(1, heads):
+        head_copy(o).wait_send()
+    for o in range(1, members):
+        rs_copy(o).wait_send()
+        ag_copy(o).wait_send()
+        bct_copy(o).wait_send()
+
+    @pl.when(z > 0)
+    def _():
+        for o in range(heads):
+            nbc_copy(o).wait_send()
+        edge_copy().wait_send()
 
 
 def shifted(block, axis, distance):
@@ -297,7 +480,7 @@
         name="carry",
     )(s_own, u_own, et)
 
-    y, gx, edge, taps_part, d_bc = pl.pallas_call(
+    y, gx, tail, edge, taps_part, d_bc = pl.pallas_call(
         functools.partial(apply_kernel, head_dim, scale),
         grid=(groups,),
         in_specs=[
@@ -306,10 +489,12 @@
             cols(tokens), cols(tokens), whole(tokens, 2 * n), whole(tokens, 2 * n),
             chunk(n, columns), chunk(n, columns),
         ],
-        out_specs=[cols(tokens), cols(tokens), cols(8), cols(8), whole(tokens, 2 * n)],
+        out_specs=[
+            cols(tokens), cols(tokens), cols(16), cols(8), cols(8), whole(tokens, 2 * n)
+        ],
         out_shape=[
-            out((tokens, channels), bf16), out((tokens, channels), bf16), out((8, channels), f32),
-            out((8, channels), f32), out((tokens, 2 * n), f32),
+            out((tokens, channels), bf16), out((tokens, channels), bf16), out((16, channels), f32),
+            out((8, channels), f32), out((8, channels), f32), out((tokens, 2 * n), bf16),
         ],
         scratch_shapes=[
             pltpu.VMEM((tokens, tokens), f32), pltpu.VMEM((tokens, tokens), f32),
@@ -323,37 +508,46 @@
         x, halo_x, conv_x, fac, cum_t, cum_r, skip, g, w, inner, slope, mapped, slope_bc, p_in, q_in
     )
 
-    d_bc = lax.psum(d_bc, "head")
-    next_rows = shifted(jnp.concatenate([edge, d_bc[:8]], axis=1), "seq", -1)
-
-    def fix(rows_out, next_part, weight):
-        last = []
-        for r in range(taps - 1):
-            row = jnp.zeros((1, weight.shape[1]), f32)
-            for k in range(r + 1):
-                row = row + weight[k : k + 1] * next_part[r - k : r - k + 1]
-            last.append(row)
-        return jnp.concatenate(last, axis=0)
-
-    fix_x = fix(gx, next_rows[:, :channels], conv_x)
-    gx = gx.at[tokens - taps + 1 :].add(fix_x.astype(bf16))
-    dpad = jnp.concatenate([d_bc, next_rows[: taps - 1, channels:]], axis=0)
-    bpad = jnp.concatenate([halo_bc[8 - taps + 1 :], bc], axis=0).astype(f32)
-    gbc = sum(conv_bc[k][None] * dpad[taps - 1 - k : taps - 1 - k + tokens] for k in range(taps))
-    taps_bc = jnp.stack([jnp.sum(d_bc * bpad[k : k + tokens], axis=0) for k in range(taps)])
-    taps_bc = jnp.pad(taps_bc, ((0, 8 - taps), (0, 0)))
-    sums = lax.psum(jnp.concatenate([taps_part, taps_bc], axis=1), ("seq", "dp"))
-    token_count = tokens * seq * lax.axis_size("dp")
-    norm_tokens = float(token_count) ** (-0.5)
-    norm_skip = float(token_count * head_dim) ** (-0.5)
-    skip_sum = jnp.sum(sums[taps, :channels].reshape(heads, head_dim), axis=1)
+    head_devices = lax.axis_size("head")
+    cores = lax.axis_size("dp")
+    members = seq * cores
+    share = 128 * -(-channels // (128 * members))
+    norm = float(tokens * members) ** (-0.5)
+    dma = pltpu.SemaphoreType.DMA
+    gbc, gx_tail, sums, taps_bc = pl.pallas_call(
+        functools.partial(finish_kernel, (seq, head_devices, cores), norm),
+        in_specs=[vmem] * 8,
+        out_specs=[vmem] * 4,
+        out_shape=[
+            out((tokens, 2 * n), bf16), out((16, channels), bf16), out((8, channels), f32),
+            out((taps, 2 * n), f32),
+        ],
+        scratch_shapes=[
+            pltpu.VMEM((members, 8, share), f32), pltpu.VMEM((members, 8, share), f32),
+            pltpu.VMEM((8, share), f32), pltpu.VMEM((members, 8, share), f32),
+            pltpu.VMEM((8, 2 * n), f32), pltpu.VMEM((members, 8, 2 * n), f32),
+            pltpu.VMEM((head_devices, tokens, 2 * n), bf16),
+            pltpu.VMEM((head_devices, 16, 2 * n), bf16), pltpu.VMEM((8, channels), f32),
+            pltpu.VMEM((tokens + 8, 2 * n), f32), pltpu.VMEM((tokens + 8, 2 * n), f32),
+        ]
+        + [dma((members,))] * 6
+        + [dma((head_devices,))] * 2
+        + [dma] * 2
+        + [dma((head_devices,))] * 2,
+        compiler_params=pltpu.CompilerParams(
+            collective_id=1, has_side_effects=True, vmem_limit_bytes=32 * 1024 * 1024
+        ),
+        name="finish",
+    )(tail, edge, taps_part, d_bc, bc, halo_bc, conv_x, conv_bc)
+    gx = lax.dynamic_update_slice(gx, gx_tail, (tokens - 16, 0))
+    skip_sum = jnp.sum(sums[taps].reshape(heads, head_dim), axis=1)
     return (
         y[None],
         gx[None],
-        gbc.astype(bf16)[None],
-        sums[:taps, :channels] * norm_tokens,
-        sums[:taps, channels:] * norm_tokens,
-        skip_sum * norm_skip,
+        gbc[None],
+        sums[:taps],
+        taps_bc,
+        skip_sum * float(head_dim) ** (-0.5),
     )
 
 

time: 172 us -> 87.2 us (0.51)
  waiting for transfers between devices: 74.5 us -> 0.01 us
  between operations: 14.3 us -> 0.88 us
  Pallas kernels: 58.2 us -> 70.8 us
  other arithmetic: 9 us -> 2.37 us
    psum x2 -> x0, waiting for transfers between devices: 69.3 us -> none  [the longest x1 47.9 us: local(): lax.psum(jnp.concatenate([taps_part, taps_bc], axis=1), ('seq', 'dp'))]
    pallas_call x0 -> x1, Pallas kernels: none -> 12.6 us  [local(): pl.pallas_call(functools.partial(finish_kernel, (seq, head_devices, cores...]
    ppermute x2 -> x1, waiting for transfers between devices: 5.09 us -> 0.01 us  [shifted(): return lax.ppermute(block, axis, route)]
    mul x3 -> x1, other arithmetic: 3.33 us -> 0.52 us  [local(): skip_sum * float(head_dim) ** (-0.5)]
    reduce_sum x2 -> x1, other arithmetic: 2.34 us -> 0.11 us  [local(): skip_sum = jnp.sum(sums[taps].reshape(heads, head_dim), axis=1)]
    ppermute x2 -> x1, starting transfers between devices: 6.2 us -> 4.92 us  [shifted(): return lax.ppermute(block, axis, route)]
  transfers between devices with their start and end apart: 4 -> 1, of which waited for: 3 -> 0; matrix products, arithmetic and copies ran while one was open for 3% -> 4% of each run, Pallas kernels for 0% -> 0%
where the time goes in v2:
time: 87.2 us; the launch traced here: 86.9 us
  Pallas kernels  70.8 us (81%)
  local copies, waits for them, and re-layouts  7.86 us (9%)
  starting transfers between devices  4.92 us (6%)
  other arithmetic  2.37 us (3%)
  between operations  0.88 us (1%)
    pallas_call x1, Pallas kernels, local(): pl.pallas_call(functools.partial(carry_kernel, seq), in_specs=[vmem] * 3,...  33.7 us
    pallas_call x1, Pallas kernels, local(): pl.pallas_call(functools.partial(apply_kernel, head_dim, scale), grid=(gr...  16 us
    pallas_call x1, Pallas kernels, local(): pl.pallas_call(functools.partial(finish_kernel, (seq, head_devices, cores...  12.6 us
    pallas_call x1, Pallas kernels, local(): pl.pallas_call(functools.partial(state_kernel, head_dim), grid=(groups,),...  8.48 us
    ppermute x1, starting transfers between devices, shifted(): return lax.ppermute(block, axis, route)  4.92 us
    unnamed x16, local copies, waits for them, and re-layouts  3.44 us
  transfers between devices with their start and end apart: 1, of which 0 were waited for; matrix products, arithmetic and copies ran while one was open for 4% of the time, Pallas kernels for 0%

profile of v2, /device:TPU:0, one launch (start us, length us, event | category | flops | bytes accessed | tf_op | source)
XLA Modules:
  0.0 86.9 jit_solution(2389663271336962767)
XLA Ops:
  0.6 0.7 slice_bitcast_fusion.1
  1.3 0.8 slice_bitcast_fusion
  2.1 4.9 %collective-permute-start = (bf16[8,2816]{1,0:T(8,128)(2,1)S(1)}, bf16[8,2816]{1,0:T(8,128)(2,1)S(1)}, u32[]{:S(2)}, u32[]{:S(2)}) collective-permute-start(bf16[8,2816]{1,0:T(8,128)(2,1)S(1)} %pad_maximum_fusion.1), channel_id=1, source_target_pairs={{0,4},{4,8},{8,12},{1,5},{5,9},{9,13},{2,6},{6,10},{10,14},{3,7},{... | collective-permute-start | bytes 135176 | tf_op jit(solution)/shard_map/ppermute | solution.py:396
  7.0 0.8 sqrt_bitcast_fusion
  7.9 0.6 reduce-window.6
  8.5 0.2 slice_reduce_fusion
  8.7 0.1 copy_bitcast_fusion
  8.8 0.1 broadcast_add_fusion
  8.9 0.2 slice_reduce_fusion.1
  9.1 0.1 sub.26
  9.2 0.1 fusion.1
  9.3 0.0 copy-start.3
  9.4 0.0 copy-start.5
  9.5 0.1 broadcast_in_dim.19
  9.5 0.1 broadcast_in_dim_reshape.3.skip_ref
  9.6 0.1 broadcast_in_dim.20
  9.7 0.1 broadcast_in_dim.21.et_ref
  9.8 0.2 copy.43.ct_ref
  10.0 0.5 copy.42.fac_ref
  10.6 8.5 %states.1 = (bf16[256,2560]{1,0:T(8,128)(2,1)S(1)}, bf16[256,2560]{1,0:T(8,128)(2,1)S(1)}, bf16[256,2560]{1,0:T(8,128)(2,1)}, bf16[5,128,512]{2,1,0:T(8,128)(2,1...) custom-call(bf16[256,2560]{1,0:T(8,128)(2,1)} %bitcast.23, ...), custom_call_target="tpu_custom_call" | custom-call | tf_op jit(solution)/shard_map/states/pallas_call | solution.py:446
  19.1 1.1 %copy-done.1 = bf16[256,2560]{1,0:T(8,128)(2,1)} copy-done((bf16[256,2560]{1,0:T(8,128)(2,1)}, bf16[256,2560]{1,0:T(8,128)(2,1)S(1)}, u32[]{:S(2)}) %copy-start.1) | copy-done | bytes 1310744
  20.1 1.1 %copy-done.2 = bf16[256,2560]{1,0:T(8,128)(2,1)} copy-done((bf16[256,2560]{1,0:T(8,128)(2,1)}, bf16[256,2560]{1,0:T(8,128)(2,1)S(1)}, u32[]{:S(2)}) %copy-start.2) | copy-done | bytes 1310744
  21.2 33.7 %carry.1 = (bf16[5,128,512]{2,1,0:T(8,128)(2,1)S(1)}, bf16[5,128,512]{2,1,0:T(8,128)(2,1)S(1)}) custom-call(bf16[5,128,512]{2,1,0:T(8,128)(2,1)S(1)} %get-tuple-element.30.s_ref, bf16[5,128,512]{2,1,0:T(8,128)(2,1)S(1)} %get-tuple-element.31.u_ref, f32[5,1,512]{2,1,0:T(1,128)S(1)} %broadcast_in_dim.21.et_ref), custom_call_target="tpu_custom_call" | custom-call | tf_op jit(solution)/shard_map/carry/pallas_call | solution.py:470
  55.0 16.0 %apply.1 = (bf16[256,2560]{1,0:T(8,128)(2,1)}, bf16[256,2560]{1,0:T(8,128)(2,1)}, f32[16,2560]{1,0:T(8,128)S(1)}, f32[8,2560]{1,0:T(8,128)S(1)}, f32[8,2560]{1,0:T(8,128)S(1)}, /*index=5*/bf16[256,256]{1,0:T(8,128)(2,1)S(1)}) custom-call(bf16[256,2560]{1,0:T(8,128)(2,1)S(1)} %bitcast.24, bf16[8,2560]{1,0:T(8,128)(2,1)S(1)} %slice.44.halo_ref, ...), custom_call_target="tpu_custom_call" | custom-call | tf_op jit(solution)/shard_map/apply/pallas_call | solution.py:483
  71.0 12.6 %finish.1 = (bf16[256,256]{1,0:T(8,128)(2,1)S(1)}, bf16[16,2560]{1,0:T(8,128)(2,1)S(1)}, f32[8,2560]{1,0:T(8,128)S(1)}, f32[4,256]{1,0:T(4,128)S(1)}) custom-call(f32[16,2560]{1,0:T(8,128)S(1)} %get-tuple-element.36.tail_ref, f32[8,2560]{1,0:T(8,128)S(1)} %get-tuple-element.37.edge_ref, f32[8,2560]{1,0:T(8,128)S(1)} %get-tuple-element.38.taps_ref, ...), custom_call_target="tpu_custom_call" | custom-call | tf_op jit(solution)/shard_map/finish/pallas_call | solution.py:517
  83.6 0.6 slice.42
  84.3 0.1 reshape_squeeze.3
  84.3 0.1 reduce_sum.9
  84.5 0.5 broadcast_multiply_fusion
  85.0 0.6 bitcast_dynamic-update-slice_fusion
  85.6 0.7 copy.49
  86.3 0.6 copy.50
  (27 shorter events, 0.3 us)
Async XLA Ops:
  0.6 8.8 %copy-start.6 = (f32[40]{0:T(128)S(1)}, f32[40]{0:T(128)}, u32[]{:S(2)}) copy-start(f32[40]{0:T(128)} %param.12) | copy-start | bytes 484
  2.1 8.4 %collective-permute-start = (bf16[8,2816]{1,0:T(8,128)(2,1)S(1)}, bf16[8,2816]{1,0:T(8,128)(2,1)S(1)}, u32[]{:S(2)}, u32[]{:S(2)}) collective-permute-start(bf16[8,2816]{1,0:T(8,128)(2,1)S(1)} %pad_maximum_fusion.1), channel_id=1, source_target_pairs={{0,4},{4,8},{8,12},{1,5},{5,9},{9,13},{2,6},{6,10},{10,14},{3,7},{... | collective-permute-start | bytes 135176 | tf_op jit(solution)/shard_map/ppermute | solution.py:396
  9.3 1.2 %copy-start.3 = (bf16[1,256,256]{2,1,0:T(8,128)(2,1)S(1)}, bf16[1,256,256]{2,1,0:T(8,128)(2,1)}, u32[]{:S(2)}) copy-start(bf16[1,256,256]{2,1,0:T(8,128)(2,1)} %param.8) | copy-start | bytes 393220
  9.3 1.2 %copy-start.4 = (f32[4,2560]{1,0:T(4,128)S(1)}, f32[4,2560]{1,0:T(4,128)}, u32[]{:S(2)}) copy-start(f32[4,2560]{1,0:T(4,128)} %cw_ref.5) | copy-start | bytes 122884
  9.4 1.2 %copy-start.5 = (f32[4,256]{1,0:T(4,128)S(1)}, f32[4,256]{1,0:T(4,128)}, u32[]{:S(2)}) copy-start(f32[4,256]{1,0:T(4,128)} %cbc_ref.3) | copy-start | bytes 12292
  19.0 1.1 %copy-start.1 = (bf16[256,2560]{1,0:T(8,128)(2,1)}, bf16[256,2560]{1,0:T(8,128)(2,1)S(1)}, u32[]{:S(2)}) copy-start(bf16[256,2560]{1,0:T(8,128)(2,1)S(1)} %get-tuple-element.25.w_ref) | copy-start | bytes 3932164
  20.1 1.1 %copy-start.2 = (bf16[256,2560]{1,0:T(8,128)(2,1)}, bf16[256,2560]{1,0:T(8,128)(2,1)S(1)}, u32[]{:S(2)}) copy-start(bf16[256,2560]{1,0:T(8,128)(2,1)S(1)} %get-tuple-element.26.inner_ref) | copy-start | bytes 3932164
  21.2 33.8 %copy-start = (bf16[1,256,2560]{2,1,0:T(8,128)(2,1)S(1)}, bf16[1,256,2560]{2,1,0:T(8,128)(2,1)}, u32[]{:S(2)}) copy-start(bf16[1,256,2560]{2,1,0:T(8,128)(2,1)} %param.7) | copy-start | bytes 3932164

commit v3 on v2

v3 whole, which is shorter than its diff:
```python
import functools

import jax
import jax.numpy as jnp
from jax import lax
from jax.experimental import pallas as pl
from jax.experimental.pallas import tpu as pltpu
from jax.sharding import PartitionSpec as P

MESH = pl.DeviceIdType.MESH
f32 = jnp.float32
bf16 = jnp.bfloat16


def dot(a, b, ca, cb):
    return lax.dot_general(a, b, (((ca,), (cb,)), ((), ())), preferred_element_type=f32)


def expander(width, columns, head_dim):
    rows = lax.broadcasted_iota(jnp.int32, (2 * width, columns), 0) % width
    cols = lax.broadcasted_iota(jnp.int32, (2 * width, columns), 1) // head_dim
    return (rows == cols).astype(f32).astype(bf16)


def conv_taps(pad_ref, weight, first, tokens):
    total = weight[0:1, :] * pad_ref[pl.ds(first, tokens), :]
    for k in range(1, weight.shape[0]):
        total = total + weight[k : k + 1, :] * pad_ref[pl.ds(first + k, tokens), :]
    return total


def silu_parts(pre):
    sigma = jax.nn.sigmoid(pre)
    return pre * sigma, sigma * (1.0 + pre * (1.0 - sigma))


def main_kernel(
    head_dim, scale, seq, lag, x_ref, x_end_ref, bc_ref, bc_end_ref, d_ref, cw_ref, cbc_ref,
    skip_ref, g_ref, y_ref, gx_ref, tail_ref, edge_ref, taps_ref, dbc_ref, bc_halo_ref,
    w_all, in_all, ds_all, ya, da, s_all, u_all, p_all, q_all, et, fac, cum_r, cum_t, halo, halo_b,
    mapped, dsbc, bp, xp, dp, sim, dsim, dbc,
    halo_send, halo_recv, send_f, recv_f, send_b, recv_b,
):
    step = pl.program_id(0)
    groups = w_all.shape[0]
    tokens, columns = x_ref.shape
    width = columns // head_dim
    n = mapped.shape[1] // 2
    taps = cw_ref.shape[0]
    first = 17 - taps
    me = lax.axis_index("seq")
    back = seq - 1 - me

    def remote(src, dst, send, recv, distance):
        return pltpu.make_async_remote_copy(
            src_ref=src, dst_ref=dst, send_sem=send, recv_sem=recv,
            device_id={"seq": me + distance}, device_id_type=MESH,
        )

    def halo_x():
        return remote(x_end_ref, halo, halo_send.at[0], halo_recv.at[0], 1)

    def halo_bc():
        return remote(bc_end_ref, halo_b, halo_send.at[1], halo_recv.at[1], 1)

    def forward(c):
        return remote(s_all.at[c], p_all.at[c], send_f.at[c], recv_f.at[c], 1)

    def backward(c):
        return remote(u_all.at[c], q_all.at[c], send_b.at[c], recv_b.at[c], -1)

    def advance(c, place, make, own, incoming):
        @pl.when(place == 0)
        def _():
            incoming[c] = jnp.zeros(incoming.shape[1:], bf16)

        @pl.when(place > 0)
        def _():
            make(c).wait_recv()

            @pl.when(place < seq - 1)
            def _():
                own[c] = (incoming[c].astype(f32) * et[c] + own[c].astype(f32)).astype(bf16)

        @pl.when(place < seq - 1)
        def _():
            make(c).start()

    def chain(at):
        cf = at - lag * me
        cb = at - lag * back

        @pl.when((cf >= 0) & (cf < groups))
        def _():
            advance(cf, me, forward, s_all, p_all)

        @pl.when((cb >= 0) & (cb < groups))
        def _():
            advance(cb, back, backward, u_all, q_all)

    @pl.when(step == 0)
    def _():
        barrier = pltpu.get_barrier_semaphore()
        for other in (lax.rem(me + 1, seq), lax.rem(me + seq - 1, seq)):
            pl.semaphore_signal(barrier, inc=1, device_id={"seq": other}, device_id_type=MESH)
        pl.semaphore_wait(barrier, 2)

        @pl.when(me < seq - 1)
        def _():
            halo_bc().start()
            halo_x().start()

        @pl.when(me == 0)
        def _():
            halo_b[...] = jnp.zeros(halo_b.shape, bf16)
            halo[...] = jnp.zeros(halo.shape, bf16)

    @pl.when(step < groups)
    def _():
        c = step
        d = d_ref[0]
        la = jnp.log(d)
        upto = (
            lax.broadcasted_iota(jnp.int32, (tokens, tokens), 0)
            <= lax.broadcasted_iota(jnp.int32, (tokens, tokens), 1)
        ).astype(f32).astype(bf16)
        rest = la
        rows = jnp.zeros(la.shape, f32)
        turned = jnp.zeros((tokens, width), f32)
        for _ in range(3):
            piece = rest.astype(bf16)
            rest = rest - piece.astype(f32)
            rows = rows + dot(piece, upto, 1, 0)
            turned = turned + dot(upto, piece, 0, 1)
        cum_r[c] = rows
        cum_t[c] = turned
        last = rows[:, tokens - 1 :]
        factors = jnp.concatenate(
            [jnp.sqrt((1.0 - d) * (1.0 + d)), jnp.exp(rows), jnp.exp(last - rows)], axis=1
        )
        high = factors.astype(bf16).astype(f32)
        both = jnp.concatenate([high, factors - high], axis=0).astype(bf16)
        fac[c] = both
        spread = dot(both, expander(width, columns, head_dim), 0, 0)
        et[c] = spread[2 * tokens - 1 : 2 * tokens]

        @pl.when(step == 0)
        def _():
            @pl.when(me > 0)
            def _():
                halo_bc().wait_recv()

            bc_halo_ref[...] = halo_b[...]
            bp[0:16, :] = halo_b[...].astype(f32)
            bp[16:, :] = bc_ref[...].astype(f32)
            value, slope = silu_parts(conv_taps(bp, cbc_ref[...], first, tokens))
            mapped[...] = value.astype(bf16)
            dsbc[...] = slope

            @pl.when(me > 0)
            def _():
                halo_x().wait_recv()

        lanes = pl.ds(pl.multiple_of(c * columns, columns), columns)
        xp[0:16, :] = halo[:, lanes].astype(f32)
        xp[16:, :] = x_ref[...].astype(f32)
        value, slope = silu_parts(conv_taps(xp, cw_ref[...], first, tokens))
        inner = value.astype(bf16)
        in_all[c] = inner
        ds_all[c] = slope.astype(bf16)
        w = (inner.astype(f32) * spread[:tokens]).astype(bf16)
        w_all[c] = w
        lead = (g_ref[...].astype(f32) * spread[tokens : 2 * tokens]).astype(bf16)
        tail = (w.astype(f32) * spread[2 * tokens :]).astype(bf16)
        s_all[c] = dot(mapped[:, :n], tail, 0, 0).astype(bf16)
        u_all[c] = dot(mapped[:, n:], lead, 0, 0).astype(bf16)

    @pl.when(step < 2 * groups)
    def _():
        chain(step)

    @pl.when((step >= groups) & (step < 2 * groups))
    def _():
        c = step - groups

        @pl.when(c == 0)
        def _():
            sim[...] = dot(mapped[:, n:], mapped[:, :n], 1, 1)
            dsim[...] = jnp.zeros_like(dsim)
            dbc[...] = jnp.zeros_like(dbc)

        lower = lax.broadcasted_iota(jnp.int32, (tokens, tokens), 0) >= lax.broadcasted_iota(
            jnp.int32, (tokens, tokens), 1
        )
        pair = 2 * head_dim
        side = lax.broadcasted_iota(jnp.int32, (1, pair), 1) < head_dim
        for j in range(width // 2):
            cols = slice(j * pair, (j + 1) * pair)
            w_pair = w_all[c, :, cols]
            g_pair = g_ref[:, cols]
            parts = []
            for e in range(2):
                h = 2 * j + e
                diff = cum_t[c, :, h : h + 1] - cum_r[c, h : h + 1, :]
                decay = jnp.exp(jnp.where(lower, diff, -1e30))
                mix = (decay * sim[...]).astype(bf16)
                mine = side if e == 0 else jnp.logical_not(side)
                g_own = jnp.where(mine, g_pair.astype(f32), 0.0).astype(bf16)
                dsim[...] += decay * dot(g_own, w_pair, 1, 1)
                parts.append((dot(mix, w_pair, 1, 0), dot(mix, g_pair, 0, 0)))
            ya[c, :, cols] = jnp.where(side, parts[0][0], parts[1][0])
            da[c, :, cols] = jnp.where(side, parts[0][1], parts[1][1])

    @pl.when(step == 2 * groups)
    def _():
        for at in range(2 * groups, groups + lag * (seq - 1)):
            chain(at)

    @pl.when(step >= 2 * groups)
    def _():
        c = step - 2 * groups
        b_mat = mapped[:, :n]
        c_mat = mapped[:, n:]
        spread = dot(fac[c], expander(width, columns, head_dim), 0, 0)
        gain = spread[:tokens]
        lead = spread[tokens : 2 * tokens]
        tail = spread[2 * tokens :]
        g = g_ref[...].astype(f32)
        inner = in_all[c].astype(f32)
        p = p_all[c]
        q = q_all[c]
        y = scale * (ya[c] + lead * dot(c_mat, p, 1, 0)) + skip_ref[...] * inner
        y_ref[...] = y.astype(bf16)
        d_w = scale * (da[c] + tail * dot(b_mat, q, 1, 0))
        d_pre = (gain * d_w + skip_ref[...] * g) * ds_all[c].astype(f32)
        dbc[:, :n] += dot((w_all[c].astype(f32) * tail).astype(bf16), q, 1, 1)
        dbc[:, n:] += dot((g * lead).astype(bf16), p, 1, 1)

        lanes = pl.ds(pl.multiple_of(c * columns, columns), columns)
        xp[0:16, :] = halo[:, lanes].astype(f32)
        xp[16:, :] = x_ref[...].astype(f32)
        dp[0:tokens, :] = d_pre
        dp[tokens:, :] = jnp.zeros((8, columns), f32)
        total = jnp.zeros((tokens, columns), f32)
        for k in range(taps):
            total = total + cw_ref[k : k + 1, :] * dp[pl.ds(taps - 1 - k, tokens), :]
            taps_ref[k : k + 1, :] = jnp.sum(
                d_pre * xp[pl.ds(first + k, tokens), :], axis=0, keepdims=True
            )
        gx_ref[...] = total.astype(bf16)
        tail_ref[...] = total[tokens - 16 :]
        taps_ref[taps : taps + 1, :] = jnp.sum(g * inner, axis=0, keepdims=True)
        taps_ref[taps + 1 :, :] = jnp.zeros((8 - taps - 1, columns), f32)
        edge_ref[...] = d_pre[0:8]

    @pl.when(step == 3 * groups - 1)
    def _():
        d_sim = dsim[...].astype(bf16)
        d_b = dbc[:, :n] + dot(d_sim, mapped[:, n:], 0, 0)
        d_c = dbc[:, n:] + dot(d_sim, mapped[:, :n], 1, 0)
        dbc_ref[:, :n] = (scale * d_b * dsbc[:, :n]).astype(bf16)
        dbc_ref[:, n:] = (scale * d_c * dsbc[:, n:]).astype(bf16)

        @pl.when(me < seq - 1)
        def _():
            halo_bc().wait_send()
            halo_x().wait_send()

        @pl.loop(0, groups)
        def _(c):
            @pl.when(me < seq - 1)
            def _():
                forward(c).wait_send()

            @pl.when(me > 0)
            def _():
                backward(c).wait_send()


def finish_kernel(
    sizes, norm, tail_ref, edge_ref, taps_ref, dbc_ref, bc_ref, bc_halo_ref, cw_ref, cbc_ref,
    gbc_ref, gx_ref, sums_ref, bsum_ref, part, rs_in, red, ag_in, bct, bct_in, head_in, next_bc,
    next_x, bp, dp, rs_send, rs_recv, ag_send, ag_recv, bc_send, bc_recv, head_send, head_recv,
    edge_send, edge_recv, nbc_send, nbc_recv,
):
    seq, heads, cores = sizes
    members = seq * cores
    z = lax.axis_index("seq")
    hd = lax.axis_index("head")
    core = lax.axis_index("dp")
    me = z * cores + core
    tokens = dbc_ref.shape[0]
    taps = cw_ref.shape[0]
    channels = taps_ref.shape[1]
    share = part.shape[2]

    def member(offset):
        at = lax.rem(me + offset, members)
        return at, {"seq": at // cores, "dp": lax.rem(at, cores)}

    barrier = pltpu.get_barrier_semaphore()
    targets = [member(o)[1] for o in range(1, members)]
    for o in range(1, heads):
        other = lax.rem(hd + o, heads)
        targets.append({"head": other})
        targets.append({"head": other, "seq": lax.rem(z + 1, seq)})
        targets.append({"head": other, "seq": lax.rem(z + seq - 1, seq)})
    for target in targets:
        pl.semaphore_signal(barrier, inc=1, device_id=target, device_id_type=MESH)

    for i in range(members):
        low = min(i * share, channels)
        high = min(low + share, channels)
        if high - low < share:
            part[i] = jnp.zeros(part.shape[1:], f32)
        if high > low:
            part[i, :, 0 : high - low] = taps_ref[:, low:high]
    pl.semaphore_wait(barrier, len(targets))

    def head_copy(o):
        return pltpu.make_async_remote_copy(
            src_ref=dbc_ref, dst_ref=head_in.at[hd], send_sem=head_send.at[o],
            recv_sem=head_recv.at[hd], device_id={"head": lax.rem(hd + o, heads)},
            device_id_type=MESH,
        )

    def nbc_copy(o):
        return pltpu.make_async_remote_copy(
            src_ref=dbc_ref.at[0:16], dst_ref=next_bc.at[hd], send_sem=nbc_send.at[o],
            recv_sem=nbc_recv.at[hd],
            device_id={"head": lax.rem(hd + o, heads), "seq": z - 1}, device_id_type=MESH,
        )

    def edge_copy():
        return pltpu.make_async_remote_copy(
            src_ref=edge_ref, dst_ref=next_x, send_sem=edge_send, recv_sem=edge_recv,
            device_id={"seq": z - 1}, device_id_type=MESH,
        )

    def rs_copy(o):
        at, device = member(o)
        return pltpu.make_async_remote_copy(
            src_ref=part.at[at], dst_ref=rs_in.at[me], send_sem=rs_send.at[o],
            recv_sem=rs_recv.at[me], device_id=device, device_id_type=MESH,
        )

    def ag_copy(o):
        return pltpu.make_async_remote_copy(
            src_ref=red, dst_ref=ag_in.at[me], send_sem=ag_send.at[o],
            recv_sem=ag_recv.at[me], device_id=member(o)[1], device_id_type=MESH,
        )

    def bct_copy(o):
        return pltpu.make_async_remote_copy(
            src_ref=bct, dst_ref=bct_in.at[me], send_sem=bc_send.at[o],
            recv_sem=bc_recv.at[me], device_id=member(o)[1], device_id_type=MESH,
        )

    def arrived(slots, sem, at, source):
        pltpu.make_async_remote_copy(
            src_ref=source, dst_ref=slots.at[at], send_sem=sem.at[at], recv_sem=sem.at[at],
            device_id=member(1)[1], device_id_type=MESH,
        ).wait_recv()

    for o in range(1, heads):
        head_copy(o).start()
    for o in range(1, members):
        rs_copy(o).start()

    @pl.when(z > 0)
    def _():
        for o in range(heads):
            nbc_copy(o).start()
        edge_copy().start()

    head_in[hd] = dbc_ref[...]
    rs_in[me] = part[me]
    bp[0:16, :] = bc_halo_ref[...].astype(f32)
    bp[16:, :] = bc_ref[...].astype(f32)

    for o in range(1, heads):
        arrived(head_in, head_recv, lax.rem(hd + o, heads), dbc_ref)
    full = head_in[0].astype(f32)
    for h in range(1, heads):
        full = full + head_in[h].astype(f32)
    for k in range(taps):
        bct[k : k + 1, :] = jnp.sum(
            full * bp[pl.ds(17 - taps + k, tokens), :], axis=0, keepdims=True
        )
    bct[taps:, :] = jnp.zeros((8 - taps, bct.shape[1]), f32)
    for o in range(1, members):
        bct_copy(o).start()
    for o in range(1, members):
        arrived(rs_in, rs_recv, lax.rem(me + o, members), part.at[0])
    total = rs_in[0]
    for i in range(1, members):
        total = total + rs_in[i]
    red[...] = total
    for o in range(1, members):
        ag_copy(o).start()
    ag_in[me] = total
    bct_in[me] = bct[...]

    dp[0:tokens, :] = full
    gx_ref[...] = tail_ref[...].astype(bf16)

    @pl.when(z == seq - 1)
    def _():
        dp[tokens : tokens + 8, :] = jnp.zeros((8, full.shape[1]), f32)

    @pl.when(z < seq - 1)
    def _():
        for o in range(heads):
            arrived(next_bc, nbc_recv, o, dbc_ref.at[0:16])
        edge_copy().wait_recv()
        rows = next_bc[0].astype(f32)
        for h in range(1, heads):
            rows = rows + next_bc[h].astype(f32)
        dp[tokens : tokens + 8, :] = rows[0:8]
        at = lax.broadcasted_iota(jnp.int32, (16, 1), 0)
        fixed = tail_ref[...]
        for r in range(taps - 1):
            row = jnp.zeros((1, channels), f32)
            for k in range(r + 1):
                row = row + cw_ref[k : k + 1, :] * next_x[r - k : r - k + 1, :]
            fixed = fixed + jnp.where(at == 16 - (taps - 1) + r, row, 0.0)
        gx_ref[...] = fixed.astype(bf16)

    grad = jnp.zeros(full.shape, f32)
    for k in range(taps):
        grad = grad + cbc_ref[k : k + 1, :] * dp[pl.ds(taps - 1 - k, tokens), :]
    gbc_ref[...] = grad.astype(bf16)

    for o in range(1, members):
        at = lax.rem(me + o, members)
        arrived(ag_in, ag_recv, at, red)
        arrived(bct_in, bc_recv, at, bct)
    bsum = bct_in[0]
    for i in range(1, members):
        bsum = bsum + bct_in[i]
    bsum_ref[...] = bsum[0:taps] * norm
    for i in range(members):
        low = min(i * share, channels)
        high = min(low + share, channels)
        if high > low:
            sums_ref[:, low:high] = ag_in[i, :, 0 : high - low] * norm

    for o in range(1, heads):
        head_copy(o).wait_send()
    for o in range(1, members):
        rs_copy(o).wait_send()
        ag_copy(o).wait_send()
        bct_copy(o).wait_send()

    @pl.when(z > 0)
    def _():
        for o in range(heads):
            nbc_copy(o).wait_send()
        edge_copy().wait_send()


def shifted(block, axis, distance):
    devices = range(lax.axis_size(axis))
    route = [(i - distance, i) for i in devices if i - distance in devices]
    return lax.ppermute(block, axis, route)


def local(x_input, bc_input, decays, conv_x, conv_bc, skip_gain, grad_out):
    x = x_input[0]
    bc = bc_input[0]
    d = decays[0]
    g = grad_out[0]
    tokens, channels = x.shape
    taps = conv_x.shape[0]
    heads = d.shape[0]
    head_dim = channels // heads
    n = bc.shape[1] // 2
    scale = float(n) ** (-0.5)
    seq = lax.axis_size("seq")
    width = next(k for k in (8, 4, 2) if heads % k == 0)
    groups = heads // width
    columns = width * head_dim

    decay_rows = d.reshape(groups, width, tokens)
    skip = jnp.repeat(skip_gain, head_dim)[None, :]

    def cols(rows):
        return pl.BlockSpec((rows, columns), lambda i: (0, lax.rem(i, groups)))

    def late(rows):
        return pl.BlockSpec((rows, columns), lambda i: (0, lax.max(i - 2 * groups, 0)))

    def whole(rows, c, at=0):
        return pl.BlockSpec((rows, c), lambda i: (at, 0))

    def out(shape, dtype):
        return jax.ShapeDtypeStruct(shape, dtype)

    dma = pltpu.SemaphoreType.DMA
    vmem = pl.BlockSpec(memory_space=pltpu.VMEM)
    wide = (groups, tokens, columns)
    y, gx, tail, edge, taps_part, d_bc, halo_bc = pl.pallas_call(
        functools.partial(main_kernel, head_dim, scale, seq, 2),
        grid=(3 * groups,),
        in_specs=[
            cols(tokens), whole(16, channels, tokens // 16 - 1), whole(tokens, 2 * n),
            whole(16, 2 * n, tokens // 16 - 1),
            pl.BlockSpec((1, width, tokens), lambda i: (lax.rem(i, groups), 0, 0)),
            cols(taps), whole(taps, 2 * n), cols(1), cols(tokens),
        ],
        out_specs=[
            late(tokens), late(tokens), late(16), late(8), late(8), whole(tokens, 2 * n),
            whole(16, 2 * n),
        ],
        out_shape=[
            out((tokens, channels), bf16), out((tokens, channels), bf16), out((16, channels), f32),
            out((8, channels), f32), out((8, channels), f32), out((tokens, 2 * n), bf16),
            out((16, 2 * n), bf16),
        ],
        scratch_shapes=[
            pltpu.VMEM(wide, bf16), pltpu.VMEM(wide, bf16), pltpu.VMEM(wide, bf16),
            pltpu.VMEM(wide, f32), pltpu.VMEM(wide, f32),
            pltpu.VMEM((groups, n, columns), bf16), pltpu.VMEM((groups, n, columns), bf16),
            pltpu.VMEM((groups, n, columns), bf16), pltpu.VMEM((groups, n, columns), bf16),
            pltpu.VMEM((groups, 1, columns), f32), pltpu.VMEM((groups, 2 * width, 3 * tokens), bf16),
            pltpu.VMEM((groups, width, tokens), f32), pltpu.VMEM((groups, tokens, width), f32),
            pltpu.VMEM((16, channels), bf16), pltpu.VMEM((16, 2 * n), bf16),
            pltpu.VMEM((tokens, 2 * n), bf16),
            pltpu.VMEM((tokens, 2 * n), f32), pltpu.VMEM((tokens + 16, 2 * n), f32),
            pltpu.VMEM((tokens + 16, columns), f32), pltpu.VMEM((tokens + 8, columns), f32),
            pltpu.VMEM((tokens, tokens), f32), pltpu.VMEM((tokens, tokens), f32),
            pltpu.VMEM((tokens, 2 * n), f32),
            dma((2,)), dma((2,)),
            dma((groups,)), dma((groups,)), dma((groups,)), dma((groups,)),
        ],
        compiler_params=pltpu.CompilerParams(
            dimension_semantics=("arbitrary",), vmem_limit_bytes=48 * 1024 * 1024,
            collective_id=0, has_side_effects=True,
        ),
        name="main",
    )(x, x, bc, bc, decay_rows, conv_x, conv_bc, skip, g)

    head_devices = lax.axis_size("head")
    cores = lax.axis_size("dp")
    members = seq * cores
    share = 128 * -(-channels // (128 * members))
    norm = float(tokens * members) ** (-0.5)
    gbc, gx_tail, sums, taps_bc = pl.pallas_call(
        functools.partial(finish_kernel, (seq, head_devices, cores), norm),
        in_specs=[vmem] * 8,
        out_specs=[vmem] * 4,
        out_shape=[
            out((tokens, 2 * n), bf16), out((16, channels), bf16), out((8, channels), f32),
            out((taps, 2 * n), f32),
        ],
        scratch_shapes=[
            pltpu.VMEM((members, 8, share), f32), pltpu.VMEM((members, 8, share), f32),
            pltpu.VMEM((8, share), f32), pltpu.VMEM((members, 8, share), f32),
            pltpu.VMEM((8, 2 * n), f32), pltpu.VMEM((members, 8, 2 * n), f32),
            pltpu.VMEM((head_devices, tokens, 2 * n), bf16),
            pltpu.VMEM((head_devices, 16, 2 * n), bf16), pltpu.VMEM((8, channels), f32),
            pltpu.VMEM((tokens + 16, 2 * n), f32), pltpu.VMEM((tokens + 8, 2 * n), f32),
        ]
        + [dma((members,))] * 6
        + [dma((head_devices,))] * 2
        + [dma] * 2
        + [dma((head_devices,))] * 2,
        compiler_params=pltpu.CompilerParams(
            collective_id=1, has_side_effects=True, vmem_limit_bytes=32 * 1024 * 1024
        ),
        name="finish",
    )(tail, edge, taps_part, d_bc, bc, halo_bc, conv_x, conv_bc)
    gx = lax.dynamic_update_slice(gx, gx_tail, (tokens - 16, 0))
    skip_sum = jnp.sum(sums[taps].reshape(heads, head_dim), axis=1)
    return (
        y[None],
        gx[None],
        gbc[None],
        sums[:taps],
        taps_bc,
        skip_sum * float(head_dim) ** (-0.5),
    )


def solution(mesh):
    return jax.shard_map(
        local,
        mesh=mesh,
        in_specs=(
            P(("groups", "dp"), "seq", "head"),
            P(("groups", "dp"), "seq", None),
            P(("groups", "dp"), "head", "seq"),
            P(None, "head"),
            P(),
            P("head"),
            P(("groups", "dp"), "seq", "head"),
        ),
        out_specs=(
            P(("groups", "dp"), "seq", "head"),
            P(("groups", "dp"), "seq", "head"),
            P(("groups", "dp"), "seq", None),
            P("groups", "head"),
            P("groups", None),
            P(("groups", "head")),
        ),
        check_vma=False,
    )
```

time: 87.2 us -> 67.5 us (0.77)
  Pallas kernels: 70.8 us -> 55.2 us
  starting transfers between devices: 4.92 us -> 0 us
  local copies, waits for them, and re-layouts: 7.86 us -> 10.7 us
  other arithmetic: 2.37 us -> 0.64 us
    pallas_call x3 -> x1, Pallas kernels: 58.2 us -> 42.7 us  [local(): pl.pallas_call(functools.partial(main_kernel, head_dim, scale, seq, 2), g...]
    unnamed x16, local copies, waits for them, and re-layouts: 3.44 us -> 9.13 us
    ppermute x1 -> x0, starting transfers between devices: 4.92 us -> none  [shifted(): return lax.ppermute(block, axis, route)]
    slice x6 -> x0, local copies, waits for them, and re-layouts: 1.82 us -> none  [the longest x1 0.78 us: local(): x[tokens - 8:]]
    another operation x5 -> x0, other arithmetic: 1.6 us -> none  [the longest x1 0.8 us: local(): jnp.stack([jnp.sqrt((1.0 - d) * (1.0 + d)), jnp.exp(cum), jnp.exp(total -...]
  transfers between devices with their start and end apart: 1 -> 0, of which waited for: 0 -> 0; matrix products, arithmetic and copies ran while one was open for 4% -> 0% of each run, Pallas kernels for 0% -> 0%
where the time goes in v3:
time: 67.5 us; the launch traced here: 67.2 us
  Pallas kernels  55.2 us (82%)
  local copies, waits for them, and re-layouts  10.7 us (16%)
  between operations  0.68 us (1%)
    pallas_call x1, Pallas kernels, local(): pl.pallas_call(functools.partial(main_kernel, head_dim, scale, seq, 2), g...  42.7 us
    pallas_call x1, Pallas kernels, local(): pl.pallas_call(functools.partial(finish_kernel, (seq, head_devices, cores...  12.4 us
    unnamed x16, local copies, waits for them, and re-layouts  9.13 us

profile of v3, /device:TPU:0, one launch (start us, length us, event | category | flops | bytes accessed | tf_op | source)
XLA Modules:
  0.0 67.2 jit_solution(16443518959242310373)
XLA Ops:
  0.6 0.7 %broadcast_in_dim.14 = f32[40,64]{1,0:T(8,128)S(1)} broadcast(f32[40]{0:T(128)} %param.12), dimensions={0} | broadcast | bytes 10400 | tf_op jit(solution)/shard_map/broadcast_in_dim | solution.py:485
  1.4 0.1 broadcast_in_dim_reshape.3.skip_ref
  1.4 0.0 copy-start
  1.5 1.3 %copy-done = bf16[1,256,2560]{2,1,0:T(8,128)(2,1)S(1)} copy-done((bf16[1,256,2560]{2,1,0:T(8,128)(2,1)S(1)}, bf16[1,256,2560]{2,1,0:T(8,128)(2,1)}, u32[]{:S(2)}) %copy-start) | copy-done | bytes 1310744
  2.8 0.0 copy-start.1
  2.8 1.3 %copy-done.1 = bf16[1,256,2560]{2,1,0:T(8,128)(2,1)S(1)} copy-done((bf16[1,256,2560]{2,1,0:T(8,128)(2,1)S(1)}, bf16[1,256,2560]{2,1,0:T(8,128)(2,1)}, u32[]{:S(2)}) %copy-start.1) | copy-done | bytes 1310744
  4.1 0.0 copy-start.2
  4.1 0.9 %copy-done.2 = bf16[1,256,256]{2,1,0:T(8,128)(2,1)S(1)} copy-done((bf16[1,256,256]{2,1,0:T(8,128)(2,1)S(1)}, bf16[1,256,256]{2,1,0:T(8,128)(2,1)}, u32[]{:S(2)}) %copy-start.2) | copy-done | bytes 131096
  5.0 0.0 copy-start.3
  5.0 0.8 %copy-done.3 = f32[4,2560]{1,0:T(4,128)S(1)} copy-done((f32[4,2560]{1,0:T(4,128)S(1)}, f32[4,2560]{1,0:T(4,128)}, u32[]{:S(2)}) %copy-start.3) | copy-done | bytes 40984
  5.8 0.0 copy-start.4
  5.8 0.8 %copy-done.4 = f32[1,40,256]{2,1,0:T(8,128)S(1)} copy-done((f32[1,40,256]{2,1,0:T(8,128)S(1)}, f32[1,40,256]{2,1,0:T(8,128)}, u32[]{:S(2)}) %copy-start.4) | copy-done | bytes 40984
  6.5 0.0 copy-start.5
  6.5 0.7 %copy-done.5 = f32[4,256]{1,0:T(4,128)S(1)} copy-done((f32[4,256]{1,0:T(4,128)S(1)}, f32[4,256]{1,0:T(4,128)}, u32[]{:S(2)}) %copy-start.5) | copy-done | bytes 4120
  7.2 42.7 %main.1 = (bf16[256,2560]{1,0:T(8,128)(2,1)S(1)}, bf16[256,2560]{1,0:T(8,128)(2,1)S(1)}, f32[16,2560]{1,0:T(8,128)S(1)}, f32[8,2560]{1,0:T(8,128)S(1)}, f32[8,25...) custom-call(bf16[256,2560]{1,0:T(8,128)(2,1)S(1)} %bitcast.9, ...), custom_call_target="tpu_custom_call" | custom-call | tf_op jit(solution)/shard_map/main/pallas_call | solution.py:502
  50.0 12.4 %finish.1 = (bf16[256,256]{1,0:T(8,128)(2,1)S(1)}, bf16[16,2560]{1,0:T(8,128)(2,1)S(1)}, f32[8,2560]{1,0:T(8,128)S(1)}, f32[4,256]{1,0:T(4,128)S(1)}) custom-call(f32[16,2560]{1,0:T(8,128)S(1)} %get-tuple-element.19.tail_ref, f32[8,2560]{1,0:T(8,128)S(1)} %get-tuple-element.20.edge_ref, f32[8,2560]{1,0:T(8,128)S(1)} %get-tuple-element.21.taps_ref, ...), custom_call_target="tpu_custom_call" | custom-call | tf_op jit(solution)/shard_map/finish/pallas_call | solution.py:548
  62.4 0.6 slice.6
  63.1 0.1 reshape_squeeze.7
  63.2 0.1 reduce_sum.9
  63.3 0.5 broadcast_multiply_fusion
  63.8 1.1 %copy.18 = bf16[1,256,2560]{2,1,0:T(8,128)(2,1)} copy(bf16[1,256,2560]{2,1,0:T(8,128)(2,1)S(1)} %bitcast.12) | data formatting | bytes 2621440
  64.9 1.1 %copy.19 = bf16[1,256,2560]{2,1,0:T(8,128)(2,1)} copy(bf16[1,256,2560]{2,1,0:T(8,128)(2,1)S(1)} %bitcast_dynamic-update-slice_fusion) | data formatting | bytes 2621440
  65.9 0.7 copy.20
  66.6 0.6 copy.21
  (2 shorter events, 0.0 us)
Async XLA Ops:
  1.4 1.3 %copy-start = (bf16[1,256,2560]{2,1,0:T(8,128)(2,1)S(1)}, bf16[1,256,2560]{2,1,0:T(8,128)(2,1)}, u32[]{:S(2)}) copy-start(bf16[1,256,2560]{2,1,0:T(8,128)(2,1)} %param.7) | copy-start | bytes 3932164
  2.8 1.3 %copy-start.1 = (bf16[1,256,2560]{2,1,0:T(8,128)(2,1)S(1)}, bf16[1,256,2560]{2,1,0:T(8,128)(2,1)}, u32[]{:S(2)}) copy-start(bf16[1,256,2560]{2,1,0:T(8,128)(2,1)} %param.13) | copy-start | bytes 3932164
  4.1 0.9 %copy-start.2 = (bf16[1,256,256]{2,1,0:T(8,128)(2,1)S(1)}, bf16[1,256,256]{2,1,0:T(8,128)(2,1)}, u32[]{:S(2)}) copy-start(bf16[1,256,256]{2,1,0:T(8,128)(2,1)} %param.8) | copy-start | bytes 393220
  5.0 0.8 %copy-start.3 = (f32[4,2560]{1,0:T(4,128)S(1)}, f32[4,2560]{1,0:T(4,128)}, u32[]{:S(2)}) copy-start(f32[4,2560]{1,0:T(4,128)} %cw_ref.3) | copy-start | bytes 122884
  5.8 0.8 %copy-start.4 = (f32[1,40,256]{2,1,0:T(8,128)S(1)}, f32[1,40,256]{2,1,0:T(8,128)}, u32[]{:S(2)}) copy-start(f32[1,40,256]{2,1,0:T(8,128)} %param.9) | copy-start | bytes 122884
  6.5 0.7 %copy-start.5 = (f32[4,256]{1,0:T(4,128)S(1)}, f32[4,256]{1,0:T(4,128)}, u32[]{:S(2)}) copy-start(f32[4,256]{1,0:T(4,128)} %cbc_ref.3) | copy-start | bytes 12292

commit v4 on v3

v4 whole, which is shorter than its diff:
```python
import functools

import jax
import jax.numpy as jnp
from jax import lax
from jax.experimental import pallas as pl
from jax.experimental.pallas import tpu as pltpu
from jax.sharding import PartitionSpec as P

MESH = pl.DeviceIdType.MESH
f32 = jnp.float32
bf16 = jnp.bfloat16


def dot(a, b, ca, cb):
    return lax.dot_general(a, b, (((ca,), (cb,)), ((), ())), preferred_element_type=f32)


def expander(width, columns, head_dim):
    rows = lax.broadcasted_iota(jnp.int32, (2 * width, columns), 0) % width
    cols = lax.broadcasted_iota(jnp.int32, (2 * width, columns), 1) // head_dim
    return (rows == cols).astype(f32).astype(bf16)


def conv_taps(pad_ref, weight, first, tokens):
    total = weight[0:1, :] * pad_ref[pl.ds(first, tokens), :]
    for k in range(1, weight.shape[0]):
        total = total + weight[k : k + 1, :] * pad_ref[pl.ds(first + k, tokens), :]
    return total


def silu_parts(pre):
    sigma = jax.nn.sigmoid(pre)
    return pre * sigma, sigma * (1.0 + pre * (1.0 - sigma))


def main_kernel(
    head_dim, scale, norm, sizes, lag, x_ref, x_end_ref, bc_ref, bc_end_ref, d_ref, cw_ref,
    cw_all_ref, cbc_ref, skip_ref, g_ref, y_ref, gx_ref, gbc_ref, sums_ref, skips_ref, bsum_ref,
    w_all, in_all, ds_all, ya, da, s_all, u_all, p_all, q_all, et, fac, cum_r, cum_t, halo, halo_b,
    mapped, dsbc, bp, xp, dp, sim, dsim, dbc,
    tails, edges, parts_x, next_x, rs_in, ag_in, bct, bct_in, dbc_out, head_in, next_bc, dbp,
    halo_send, halo_recv, send_f, recv_f, send_b, recv_b,
    edge_send, edge_recv, rs_send, rs_recv, ag_send, ag_recv, bct_send, bct_recv,
    head_send, head_recv, nbc_send, nbc_recv,
):
    step = pl.program_id(0)
    groups = w_all.shape[0]
    tokens, columns = x_ref.shape
    width = columns // head_dim
    n = mapped.shape[1] // 2
    taps = cw_ref.shape[0]
    first = 17 - taps
    seq, heads, cores = sizes
    members = seq * cores
    me = lax.axis_index("seq")
    back = seq - 1 - me
    hd = lax.axis_index("head")
    place = me * cores + lax.axis_index("dp")

    def member(offset):
        at = lax.rem(place + offset, members)
        return at, {"seq": at // cores, "dp": lax.rem(at, cores)}

    def copy(src, dst, send, recv, device):
        return pltpu.make_async_remote_copy(
            src_ref=src, dst_ref=dst, send_sem=send, recv_sem=recv, device_id=device,
            device_id_type=MESH,
        )

    def head_copy(o):
        return copy(
            dbc_out, head_in.at[hd], head_send.at[o], head_recv.at[hd],
            {"head": lax.rem(hd + o, heads)},
        )

    def nbc_copy(o):
        return copy(
            dbc_out.at[0:16], next_bc.at[hd], nbc_send.at[o], nbc_recv.at[hd],
            {"head": lax.rem(hd + o, heads), "seq": me - 1},
        )

    def edge_copy(c):
        return copy(
            edges.at[c], next_x.at[c], edge_send.at[c], edge_recv.at[c], {"seq": me - 1}
        )

    def rs_copy(c):
        owner = lax.rem(c, members)
        return copy(
            parts_x.at[c], rs_in.at[c, place], rs_send.at[c], rs_recv.at[c, place],
            {"seq": owner // cores, "dp": lax.rem(owner, cores)},
        )

    def ag_copy(c, o):
        return copy(ag_in.at[c], ag_in.at[c], ag_send.at[c, o], ag_recv.at[c], member(o)[1])

    def bct_copy(o):
        return copy(bct, bct_in.at[place], bct_send.at[o], bct_recv.at[place], member(o)[1])

    def arrived(dst, sem, source):
        copy(source, dst, sem, sem, member(1)[1]).wait_recv()

    def remote(src, dst, send, recv, distance):
        return pltpu.make_async_remote_copy(
            src_ref=src, dst_ref=dst, send_sem=send, recv_sem=recv,
            device_id={"seq": me + distance}, device_id_type=MESH,
        )

    def halo_x():
        return remote(x_end_ref, halo, halo_send.at[0], halo_recv.at[0], 1)

    def halo_bc():
        return remote(bc_end_ref, halo_b, halo_send.at[1], halo_recv.at[1], 1)

    def forward(c):
        return remote(s_all.at[c], p_all.at[c], send_f.at[c], recv_f.at[c], 1)

    def backward(c):
        return remote(u_all.at[c], q_all.at[c], send_b.at[c], recv_b.at[c], -1)

    def advance(c, hops, make, own, incoming):
        @pl.when(hops == 0)
        def _():
            incoming[c] = jnp.zeros(incoming.shape[1:], bf16)

        @pl.when(hops > 0)
        def _():
            make(c).wait_recv()

            @pl.when(hops < seq - 1)
            def _():
                own[c] = (incoming[c].astype(f32) * et[c] + own[c].astype(f32)).astype(bf16)

        @pl.when(hops < seq - 1)
        def _():
            make(c).start()

    def chain(at):
        cf = at - lag * me
        cb = at - lag * back

        @pl.when((cf >= 0) & (cf < groups))
        def _():
            advance(cf, me, forward, s_all, p_all)

        @pl.when((cb >= 0) & (cb < groups))
        def _():
            advance(cb, back, backward, u_all, q_all)

    @pl.when(step == 0)
    def _():
        barrier = pltpu.get_barrier_semaphore()
        targets = [member(o)[1] for o in range(1, members)]
        for o in range(1, heads):
            other = lax.rem(hd + o, heads)
            targets.append({"head": other})
            targets.append({"head": other, "seq": lax.rem(me + 1, seq)})
            targets.append({"head": other, "seq": lax.rem(me + seq - 1, seq)})
        for target in targets:
            pl.semaphore_signal(barrier, inc=1, device_id=target, device_id_type=MESH)
        pl.semaphore_wait(barrier, len(targets))

        @pl.when(me < seq - 1)
        def _():
            halo_bc().start()
            halo_x().start()

        @pl.when(me == 0)
        def _():
            halo_b[...] = jnp.zeros(halo_b.shape, bf16)
            halo[...] = jnp.zeros(halo.shape, bf16)

    @pl.when(step < groups)
    def _():
        c = step
        d = d_ref[0]
        la = jnp.log(d)
        upto = (
            lax.broadcasted_iota(jnp.int32, (tokens, tokens), 0)
            <= lax.broadcasted_iota(jnp.int32, (tokens, tokens), 1)
        ).astype(f32).astype(bf16)
        rest = la
        rows = jnp.zeros(la.shape, f32)
        turned = jnp.zeros((tokens, width), f32)
        for _ in range(3):
            piece = rest.astype(bf16)
            rest = rest - piece.astype(f32)
            rows = rows + dot(piece, upto, 1, 0)
            turned = turned + dot(upto, piece, 0, 1)
        cum_r[c] = rows
        cum_t[c] = turned
        last = rows[:, tokens - 1 :]
        factors = jnp.concatenate(
            [jnp.sqrt((1.0 - d) * (1.0 + d)), jnp.exp(rows), jnp.exp(last - rows)], axis=1
        )
        high = factors.astype(bf16).astype(f32)
        both = jnp.concatenate([high, factors - high], axis=0).astype(bf16)
        fac[c] = both
        spread = dot(both, expander(width, columns, head_dim), 0, 0)
        et[c] = spread[2 * tokens - 1 : 2 * tokens]

        @pl.when(step == 0)
        def _():
            @pl.when(me > 0)
            def _():
                halo_bc().wait_recv()

            bp[0:16, :] = halo_b[...].astype(f32)
            bp[16:, :] = bc_ref[...].astype(f32)
            value, slope = silu_parts(conv_taps(bp, cbc_ref[...], first, tokens))
            mapped[...] = value.astype(bf16)
            dsbc[...] = slope

            @pl.when(me > 0)
            def _():
                halo_x().wait_recv()

        lanes = pl.ds(pl.multiple_of(c * columns, columns), columns)
        xp[0:16, :] = halo[:, lanes].astype(f32)
        xp[16:, :] = x_ref[...].astype(f32)
        value, slope = silu_parts(conv_taps(xp, cw_ref[...], first, tokens))
        inner = value.astype(bf16)
        in_all[c] = inner
        ds_all[c] = slope.astype(bf16)
        w = (inner.astype(f32) * spread[:tokens]).astype(bf16)
        w_all[c] = w
        lead = (g_ref[...].astype(f32) * spread[tokens : 2 * tokens]).astype(bf16)
        tail = (w.astype(f32) * spread[2 * tokens :]).astype(bf16)
        s_all[c] = dot(mapped[:, :n], tail, 0, 0).astype(bf16)
        u_all[c] = dot(mapped[:, n:], lead, 0, 0).astype(bf16)

    @pl.when(step < 2 * groups)
    def _():
        chain(step)

    @pl.when((step >= groups) & (step < 2 * groups))
    def _():
        c = step - groups

        @pl.when(c == 0)
        def _():
            sim[...] = dot(mapped[:, n:], mapped[:, :n], 1, 1)
            dsim[...] = jnp.zeros_like(dsim)
            dbc[...] = jnp.zeros_like(dbc)

        lower = lax.broadcasted_iota(jnp.int32, (tokens, tokens), 0) >= lax.broadcasted_iota(
            jnp.int32, (tokens, tokens), 1
        )
        pair = 2 * head_dim
        side = lax.broadcasted_iota(jnp.int32, (1, pair), 1) < head_dim
        for j in range(width // 2):
            cols = slice(j * pair, (j + 1) * pair)
            w_pair = w_all[c, :, cols]
            g_pair = g_ref[:, cols]
            parts = []
            for e in range(2):
                h = 2 * j + e
                diff = cum_t[c, :, h : h + 1] - cum_r[c, h : h + 1, :]
                decay = jnp.exp(jnp.where(lower, diff, -1e30))
                mix = (decay * sim[...]).astype(bf16)
                mine = side if e == 0 else jnp.logical_not(side)
                g_own = jnp.where(mine, g_pair.astype(f32), 0.0).astype(bf16)
                dsim[...] += decay * dot(g_own, w_pair, 1, 1)
                parts.append((dot(mix, w_pair, 1, 0), dot(mix, g_pair, 0, 0)))
            ya[c, :, cols] = jnp.where(side, parts[0][0], parts[1][0])
            da[c, :, cols] = jnp.where(side, parts[0][1], parts[1][1])

    @pl.when(step == 2 * groups)
    def _():
        for at in range(2 * groups, groups + lag * (seq - 1)):
            chain(at)

    @pl.when(step >= 2 * groups)
    def _():
        c = step - 2 * groups
        b_mat = mapped[:, :n]
        c_mat = mapped[:, n:]
        spread = dot(fac[c], expander(width, columns, head_dim), 0, 0)
        gain = spread[:tokens]
        lead = spread[tokens : 2 * tokens]
        tail = spread[2 * tokens :]
        g = g_ref[...].astype(f32)
        inner = in_all[c].astype(f32)
        p = p_all[c]
        q = q_all[c]
        y = scale * (ya[c] + lead * dot(c_mat, p, 1, 0)) + skip_ref[...] * inner
        y_ref[...] = y.astype(bf16)
        d_w = scale * (da[c] + tail * dot(b_mat, q, 1, 0))
        d_pre = (gain * d_w + skip_ref[...] * g) * ds_all[c].astype(f32)
        dbc[:, :n] += dot((w_all[c].astype(f32) * tail).astype(bf16), q, 1, 1)
        dbc[:, n:] += dot((g * lead).astype(bf16), p, 1, 1)

        lanes = pl.ds(pl.multiple_of(c * columns, columns), columns)
        xp[0:16, :] = halo[:, lanes].astype(f32)
        xp[16:, :] = x_ref[...].astype(f32)
        dp[0:tokens, :] = d_pre
        dp[tokens:, :] = jnp.zeros((8, columns), f32)
        total = jnp.zeros((tokens, columns), f32)
        for k in range(taps):
            total = total + cw_ref[k : k + 1, :] * dp[pl.ds(taps - 1 - k, tokens), :]
            parts_x[c, k : k + 1, :] = jnp.sum(
                d_pre * xp[pl.ds(first + k, tokens), :], axis=0, keepdims=True
            )
        gx_ref[:, lanes] = total.astype(bf16)
        tails[c] = total[tokens - 16 :]
        parts_x[c, taps : taps + 1, :] = jnp.sum(g * inner, axis=0, keepdims=True)
        parts_x[c, taps + 1 :, :] = jnp.zeros((8 - taps - 1, columns), f32)
        edges[c] = d_pre[0:8]

        @pl.when(me > 0)
        def _():
            edge_copy(c).start()

        @pl.when(place != lax.rem(c, members))
        def _():
            rs_copy(c).start()

    @pl.when(step == 3 * groups - 1)
    def _():
        d_sim = dsim[...].astype(bf16)
        d_b = dbc[:, :n] + dot(d_sim, mapped[:, n:], 0, 0)
        d_c = dbc[:, n:] + dot(d_sim, mapped[:, :n], 1, 0)
        dbc_out[:, :n] = (scale * d_b * dsbc[:, :n]).astype(bf16)
        dbc_out[:, n:] = (scale * d_c * dsbc[:, n:]).astype(bf16)
        for o in range(1, heads):
            head_copy(o).start()

        @pl.when(me > 0)
        def _():
            for o in range(heads):
                nbc_copy(o).start()

        head_in[hd] = dbc_out[...]
        for c in range(groups):
            @pl.when(place == c % members)
            def _():
                for o in range(1, members):
                    at = lax.rem(place + o, members)
                    arrived(rs_in.at[c, at], rs_recv.at[c, at], parts_x.at[c])
                rs_in[c, c % members] = parts_x[c]
                total = rs_in[c, 0]
                for i in range(1, members):
                    total = total + rs_in[c, i]
                ag_in[c] = total
                for o in range(1, members):
                    ag_copy(c, o).start()

        for o in range(1, heads):
            at = lax.rem(hd + o, heads)
            arrived(head_in.at[at], head_recv.at[at], dbc_out)
        full = head_in[0].astype(f32)
        for h in range(1, heads):
            full = full + head_in[h].astype(f32)
        for k in range(taps):
            bct[k : k + 1, :] = jnp.sum(
                full * bp[pl.ds(first + k, tokens), :], axis=0, keepdims=True
            )
        bct[taps:, :] = jnp.zeros((8 - taps, bct.shape[1]), f32)
        for o in range(1, members):
            bct_copy(o).start()
        bct_in[place] = bct[...]
        dbp[0:tokens, :] = full

        @pl.when(me == seq - 1)
        def _():
            dbp[tokens:, :] = jnp.zeros((8, full.shape[1]), f32)

        @pl.when(me < seq - 1)
        def _():
            at = lax.broadcasted_iota(jnp.int32, (16, 1), 0)
            for c in range(groups):
                edge_copy(c).wait_recv()
                cols = slice(c * columns, (c + 1) * columns)
                fixed = tails[c]
                for r in range(taps - 1):
                    row = jnp.zeros((1, columns), f32)
                    for k in range(r + 1):
                        row = row + cw_all_ref[k : k + 1, cols] * next_x[c, r - k : r - k + 1, :]
                    fixed = fixed + jnp.where(at == 16 - (taps - 1) + r, row, 0.0)
                gx_ref[tokens - 16 :, cols] = fixed.astype(bf16)
            for o in range(heads):
                arrived(next_bc.at[o], nbc_recv.at[o], dbc_out.at[0:16])
            rows = next_bc[0].astype(f32)
            for h in range(1, heads):
                rows = rows + next_bc[h].astype(f32)
            dbp[tokens:, :] = rows[0:8]

        grad = jnp.zeros(full.shape, f32)
        for k in range(taps):
            grad = grad + cbc_ref[k : k + 1, :] * dbp[pl.ds(taps - 1 - k, tokens), :]
        gbc_ref[...] = grad.astype(bf16)

        for c in range(groups):
            @pl.when(place != c % members)
            def _():
                arrived(ag_in.at[c], ag_recv.at[c], ag_in.at[c])
            cols = slice(c * columns, (c + 1) * columns)
            sums_ref[:, cols] = ag_in[c, 0:taps] * norm
            skips_ref[:, cols] = ag_in[c, taps : taps + 1] * norm
        for o in range(1, members):
            at = lax.rem(place + o, members)
            arrived(bct_in.at[at], bct_recv.at[at], bct)
        bsum = bct_in[0]
        for i in range(1, members):
            bsum = bsum + bct_in[i]
        bsum_ref[...] = bsum[0:taps] * norm

        for o in range(1, heads):
            head_copy(o).wait_send()
        for o in range(1, members):
            bct_copy(o).wait_send()
        for c in range(groups):
            @pl.when(place == c % members)
            def _():
                for o in range(1, members):
                    ag_copy(c, o).wait_send()

            @pl.when(place != c % members)
            def _():
                rs_copy(c).wait_send()

        @pl.when(me > 0)
        def _():
            for o in range(heads):
                nbc_copy(o).wait_send()
            for c in range(groups):
                edge_copy(c).wait_send()

        @pl.when(me < seq - 1)
        def _():
            halo_bc().wait_send()
            halo_x().wait_send()

        @pl.loop(0, groups)
        def _(c):
            @pl.when(me < seq - 1)
            def _():
                forward(c).wait_send()

            @pl.when(me > 0)
            def _():
                backward(c).wait_send()


def local(x_input, bc_input, decays, conv_x, conv_bc, skip_gain, grad_out):
    x = x_input[0]
    bc = bc_input[0]
    d = decays[0]
    g = grad_out[0]
    tokens, channels = x.shape
    taps = conv_x.shape[0]
    heads = d.shape[0]
    head_dim = channels // heads
    n = bc.shape[1] // 2
    scale = float(n) ** (-0.5)
    seq = lax.axis_size("seq")
    width = next(k for k in (8, 4, 2) if heads % k == 0)
    groups = heads // width
    columns = width * head_dim

    decay_rows = d.reshape(groups, width, tokens)
    skip = jnp.repeat(skip_gain, head_dim)[None, :]

    def cols(rows):
        return pl.BlockSpec((rows, columns), lambda i: (0, lax.rem(i, groups)))

    def late(rows):
        return pl.BlockSpec((rows, columns), lambda i: (0, lax.max(i - 2 * groups, 0)))

    def whole(rows, c, at=0):
        return pl.BlockSpec((rows, c), lambda i: (at, 0))

    def out(shape, dtype):
        return jax.ShapeDtypeStruct(shape, dtype)

    dma = pltpu.SemaphoreType.DMA
    wide = (groups, tokens, columns)
    head_devices = lax.axis_size("head")
    cores = lax.axis_size("dp")
    members = seq * cores
    norm = float(tokens * members) ** (-0.5)
    sizes = (seq, head_devices, cores)
    block = (groups, 8, columns)
    y, gx, gbc, sums, skips, taps_bc = pl.pallas_call(
        functools.partial(main_kernel, head_dim, scale, norm, sizes, 2),
        grid=(3 * groups,),
        in_specs=[
            cols(tokens), whole(16, channels, tokens // 16 - 1), whole(tokens, 2 * n),
            whole(16, 2 * n, tokens // 16 - 1),
            pl.BlockSpec((1, width, tokens), lambda i: (lax.rem(i, groups), 0, 0)),
            cols(taps), whole(taps, channels), whole(taps, 2 * n), cols(1), cols(tokens),
        ],
        out_specs=[
            late(tokens), whole(tokens, channels), whole(tokens, 2 * n), whole(taps, channels),
            whole(1, channels), whole(taps, 2 * n),
        ],
        out_shape=[
            out((tokens, channels), bf16), out((tokens, channels), bf16),
            out((tokens, 2 * n), bf16), out((taps, channels), f32), out((1, channels), f32),
            out((taps, 2 * n), f32),
        ],
        scratch_shapes=[
            pltpu.VMEM(wide, bf16), pltpu.VMEM(wide, bf16), pltpu.VMEM(wide, bf16),
            pltpu.VMEM(wide, f32), pltpu.VMEM(wide, f32),
            pltpu.VMEM((groups, n, columns), bf16), pltpu.VMEM((groups, n, columns), bf16),
            pltpu.VMEM((groups, n, columns), bf16), pltpu.VMEM((groups, n, columns), bf16),
            pltpu.VMEM((groups, 1, columns), f32), pltpu.VMEM((groups, 2 * width, 3 * tokens), bf16),
            pltpu.VMEM((groups, width, tokens), f32), pltpu.VMEM((groups, tokens, width), f32),
            pltpu.VMEM((16, channels), bf16), pltpu.VMEM((16, 2 * n), bf16),
            pltpu.VMEM((tokens, 2 * n), bf16),
            pltpu.VMEM((tokens, 2 * n), f32), pltpu.VMEM((tokens + 16, 2 * n), f32),
            pltpu.VMEM((tokens + 16, columns), f32), pltpu.VMEM((tokens + 8, columns), f32),
            pltpu.VMEM((tokens, tokens), f32), pltpu.VMEM((tokens, tokens), f32),
            pltpu.VMEM((tokens, 2 * n), f32),
            pltpu.VMEM((groups, 16, columns), f32), pltpu.VMEM(block, f32),
            pltpu.VMEM(block, f32), pltpu.VMEM(block, f32),
            pltpu.VMEM((groups, members, 8, columns), f32), pltpu.VMEM(block, f32),
            pltpu.VMEM((8, 2 * n), f32), pltpu.VMEM((members, 8, 2 * n), f32),
            pltpu.VMEM((tokens, 2 * n), bf16), pltpu.VMEM((head_devices, tokens, 2 * n), bf16),
            pltpu.VMEM((head_devices, 16, 2 * n), bf16), pltpu.VMEM((tokens + 8, 2 * n), f32),
            dma((2,)), dma((2,)),
            dma((groups,)), dma((groups,)), dma((groups,)), dma((groups,)),
            dma((groups,)), dma((groups,)), dma((groups,)), dma((groups, members)),
            dma((groups, members)), dma((groups,)), dma((members,)), dma((members,)),
            dma((head_devices,)), dma((head_devices,)), dma((head_devices,)),
            dma((head_devices,)),
        ],
        compiler_params=pltpu.CompilerParams(
            dimension_semantics=("arbitrary",), vmem_limit_bytes=60 * 1024 * 1024,
            collective_id=0, has_side_effects=True,
        ),
        name="main",
    )(x, x, bc, bc, decay_rows, conv_x, conv_x, conv_bc, skip, g)

    skip_sum = jnp.sum(skips.reshape(heads, head_dim), axis=1)
    return (
        y[None],
        gx[None],
        gbc[None],
        sums,
        taps_bc,
        skip_sum * float(head_dim) ** (-0.5),
    )


def solution(mesh):
    return jax.shard_map(
        local,
        mesh=mesh,
        in_specs=(
            P(("groups", "dp"), "seq", "head"),
            P(("groups", "dp"), "seq", None),
            P(("groups", "dp"), "head", "seq"),
            P(None, "head"),
            P(),
            P("head"),
            P(("groups", "dp"), "seq", "head"),
        ),
        out_specs=(
            P(("groups", "dp"), "seq", "head"),
            P(("groups", "dp"), "seq", "head"),
            P(("groups", "dp"), "seq", None),
            P("groups", "head"),
            P("groups", None),
            P(("groups", "head")),
        ),
        check_vma=False,
    )
```

time: 67.5 us -> 64.5 us (0.956)
  local copies, waits for them, and re-layouts: 10.7 us -> 6.98 us
  other arithmetic: 0.64 us -> 1.37 us
    unnamed x16 -> x13, local copies, waits for them, and re-layouts: 9.13 us -> 5.5 us
    pallas_call x0 -> x1, other arithmetic: none -> 0.73 us  [local(): pl.pallas_call(functools.partial(main_kernel, head_dim, scale, norm, size...]
    pallas_call x2 -> x1, Pallas kernels: 55.2 us -> 55.2 us  [local(): pl.pallas_call(functools.partial(main_kernel, head_dim, scale, norm, size...]
where the time goes in v4:
time: 64.5 us; the launch traced here: 64.2 us
  Pallas kernels  55.2 us (86%)
  local copies, waits for them, and re-layouts  6.98 us (11%)
  other arithmetic  1.37 us (2%)
  between operations  0.65 us (1%)
    pallas_call x1, Pallas kernels, local(): pl.pallas_call(functools.partial(main_kernel, head_dim, scale, norm, size...  55.2 us
    unnamed x13, local copies, waits for them, and re-layouts  5.5 us

profile of v4, /device:TPU:0, one launch (start us, length us, event | category | flops | bytes accessed | tf_op | source)
XLA Modules:
  0.0 64.2 jit_solution(7904260626893268833)
XLA Ops:
  0.6 0.7 %broadcast_in_dim.12 = f32[40,64]{1,0:T(8,128)S(1)} broadcast(f32[40]{0:T(128)} %param.12), dimensions={0} | broadcast | bytes 10400 | tf_op jit(solution)/shard_map/broadcast_in_dim | solution.py:463
  1.4 0.7 %broadcast_in_dim_reshape.3.skip_ref = f32[1,2560]{1,0:T(1,128)} reshape(f32[40,64]{1,0:T(8,128)S(1)} %broadcast_in_dim.12) | data formatting | bytes 20480 | tf_op jit(solution)/shard_map/broadcast_in_dim;reshape | solution.py:463
  2.0 55.2 %main.1 = (bf16[256,2560]{1,0:T(8,128)(2,1)}, bf16[256,2560]{1,0:T(8,128)(2,1)}, bf16[256,256]{1,0:T(8,128)(2,1)}, f32[4,2560]{1,0:T(4,128)}, f32[1,2560]{1,0:T(1,128)}, /*index=5*/f32[4,256]{1,0:T(4,128)}) custom-call(bf16[256,2560]{1,0:T(8,128)(2,1)} %bitcast.7, bf16[256,2560]{1,0:T(8,128)(2,1)} %bitcast.8, bf16[256,256]{1,0:T(8,128)(2,1)} %bitcast.12, ...), custom_call_target="tpu_custom_call" | custom-call | tf_op jit(solution)/shard_map/main/pallas_call | solution.py:485
  57.3 0.7 %reduce = f32[2560]{0:T(1024)S(1)} reduce(f32[1,2560]{1,0:T(1,128)} %get-tuple-element.17, f32[]{:T(128)} %constant.8), dimensions={0}, to_apply=%get-tuple-element.17.reduce_sub_computation | reduce | bytes 20484 | tf_op jit(solution)/shard_map/main/pallas_call | solution.py:485
  58.0 0.1 reshape.15
  58.1 0.1 reduce_sum.9
  58.2 0.5 broadcast_multiply_fusion
  58.7 0.0 copy-start
  58.7 2.6 %copy.18 = bf16[1,256,2560]{2,1,0:T(8,128)(2,1)} copy(bf16[1,256,2560]{2,1,0:T(8,128)(2,1)} %bitcast.11) | data formatting | bytes 2621440
  61.3 0.0 copy-done
  61.3 0.0 copy-start.1
  61.3 0.0 copy-start.2
  61.3 0.0 copy-start.3
  61.3 1.1 %copy.19 = bf16[1,256,2560]{2,1,0:T(8,128)(2,1)} copy(bf16[1,256,2560]{2,1,0:T(8,128)(2,1)S(1)} %bitcast.10) | data formatting | bytes 2621440
  62.3 0.0 copy-done.1
  62.3 0.7 %copy.20 = bf16[1,256,256]{2,1,0:T(8,128)(2,1)} copy(bf16[1,256,256]{2,1,0:T(8,128)(2,1)S(1)} %bitcast.14) | data formatting | bytes 262144
  63.0 0.0 copy-done.2
  63.0 0.6 copy.21
  63.6 0.0 copy-done.3
  63.6 0.6 copy.22
Async XLA Ops:
  58.7 2.6 %copy-start = (bf16[256,2560]{1,0:T(8,128)(2,1)S(1)}, bf16[256,2560]{1,0:T(8,128)(2,1)}, u32[]{:S(2)}) copy-start(bf16[256,2560]{1,0:T(8,128)(2,1)} %get-tuple-element.13) | copy-start | bytes 3932164
  61.3 1.1 %copy-start.1 = (bf16[256,256]{1,0:T(8,128)(2,1)S(1)}, bf16[256,256]{1,0:T(8,128)(2,1)}, u32[]{:S(2)}) copy-start(bf16[256,256]{1,0:T(8,128)(2,1)} %get-tuple-element.14) | copy-start | bytes 393220
  61.3 1.7 %copy-start.2 = (f32[4,2560]{1,0:T(4,128)S(1)}, f32[4,2560]{1,0:T(4,128)}, u32[]{:S(2)}) copy-start(f32[4,2560]{1,0:T(4,128)} %get-tuple-element.27) | copy-start | bytes 122884
  61.3 2.3 %copy-start.3 = (f32[4,256]{1,0:T(4,128)S(1)}, f32[4,256]{1,0:T(4,128)}, u32[]{:S(2)}) copy-start(f32[4,256]{1,0:T(4,128)} %get-tuple-element.28) | copy-start | bytes 12292

commit v5 on v4

--- a/solution.py
+++ b/solution.py
@@ -282,12 +282,16 @@
         tail = spread[2 * tokens :]
         g = g_ref[...].astype(f32)
         inner = in_all[c].astype(f32)
+        lane = lax.broadcasted_iota(jnp.int32, (1, columns), 1) // head_dim
+        skip = jnp.zeros((1, columns), f32)
+        for j in range(width):
+            skip = jnp.where(lane == j, skip_ref[c * width + j], skip)
         p = p_all[c]
         q = q_all[c]
-        y = scale * (ya[c] + lead * dot(c_mat, p, 1, 0)) + skip_ref[...] * inner
+        y = scale * (ya[c] + lead * dot(c_mat, p, 1, 0)) + skip * inner
         y_ref[...] = y.astype(bf16)
         d_w = scale * (da[c] + tail * dot(b_mat, q, 1, 0))
-        d_pre = (gain * d_w + skip_ref[...] * g) * ds_all[c].astype(f32)
+        d_pre = (gain * d_w + skip * g) * ds_all[c].astype(f32)
         dbc[:, :n] += dot((w_all[c].astype(f32) * tail).astype(bf16), q, 1, 1)
         dbc[:, n:] += dot((g * lead).astype(bf16), p, 1, 1)
 
@@ -460,7 +464,6 @@
     columns = width * head_dim
 
     decay_rows = d.reshape(groups, width, tokens)
-    skip = jnp.repeat(skip_gain, head_dim)[None, :]
 
     def cols(rows):
         return pl.BlockSpec((rows, columns), lambda i: (0, lax.rem(i, groups)))
@@ -489,7 +492,8 @@
             cols(tokens), whole(16, channels, tokens // 16 - 1), whole(tokens, 2 * n),
             whole(16, 2 * n, tokens // 16 - 1),
             pl.BlockSpec((1, width, tokens), lambda i: (lax.rem(i, groups), 0, 0)),
-            cols(taps), whole(taps, channels), whole(taps, 2 * n), cols(1), cols(tokens),
+            cols(taps), whole(taps, channels), whole(taps, 2 * n),
+            pl.BlockSpec(memory_space=pltpu.SMEM), cols(tokens),
         ],
         out_specs=[
             late(tokens), whole(tokens, channels), whole(tokens, 2 * n), whole(taps, channels),
@@ -531,7 +535,7 @@
             collective_id=0, has_side_effects=True,
         ),
         name="main",
-    )(x, x, bc, bc, decay_rows, conv_x, conv_x, conv_bc, skip, g)
+    )(x, x, bc, bc, decay_rows, conv_x, conv_x, conv_bc, skip_gain, g)
 
     skip_sum = jnp.sum(skips.reshape(heads, head_dim), axis=1)
     return (

time: 64.5 us -> 63.2 us (0.980)
  local copies, waits for them, and re-layouts: 6.98 us -> 5.57 us
    broadcast_in_dim x1 -> x0, local copies, waits for them, and re-layouts: 0.73 us -> none  [local(): skip = jnp.repeat(skip_gain, head_dim)[None, :]]
    another operation x1 -> x0, local copies, waits for them, and re-layouts: 0.68 us -> none  [local(): skip = jnp.repeat(skip_gain, head_dim)[None, :]]
where the time goes in v5:
time: 63.2 us; the launch traced here: 62.9 us
  Pallas kernels  55.3 us (88%)
  local copies, waits for them, and re-layouts  5.57 us (9%)
  other arithmetic  1.37 us (2%)
  between operations  0.66 us (1%)
    pallas_call x1, Pallas kernels, local(): pl.pallas_call(functools.partial(main_kernel, head_dim, scale, norm, size...  55.3 us
    unnamed x13, local copies, waits for them, and re-layouts  5.5 us

profile of v5, /device:TPU:0, one launch (start us, length us, event | category | flops | bytes accessed | tf_op | source)
XLA Modules:
  0.0 62.9 jit_solution(6369942686271123597)
XLA Ops:
  0.6 55.3 %main.1 = (bf16[256,2560]{1,0:T(8,128)(2,1)}, bf16[256,2560]{1,0:T(8,128)(2,1)}, bf16[256,256]{1,0:T(8,128)(2,1)}, f32[4,2560]{1,0:T(4,128)}, f32[1,2560]{1,0:T(1,128)}, /*index=5*/f32[4,256]{1,0:T(4,128)}) custom-call(bf16[256,2560]{1,0:T(8,128)(2,1)} %bitcast.7, bf16[256,2560]{1,0:T(8,128)(2,1)} %bitcast.8, bf16[256,256]{1,0:T(8,128)(2,1)} %bitcast.12, ...), custom_call_target="tpu_custom_call" | custom-call | tf_op jit(solution)/shard_map/main/pallas_call | solution.py:488
  56.0 0.7 %reduce = f32[2560]{0:T(1024)S(1)} reduce(f32[1,2560]{1,0:T(1,128)} %get-tuple-element.17, f32[]{:T(128)} %constant.8), dimensions={0}, to_apply=%get-tuple-element.17.reduce_sub_computation | reduce | bytes 20484 | tf_op jit(solution)/shard_map/main/pallas_call | solution.py:488
  56.7 0.1 reshape.15
  56.8 0.1 reduce_sum.9
  56.9 0.5 broadcast_multiply_fusion
  57.4 0.0 copy-start
  57.4 2.6 %copy.18 = bf16[1,256,2560]{2,1,0:T(8,128)(2,1)} copy(bf16[1,256,2560]{2,1,0:T(8,128)(2,1)} %bitcast.10) | data formatting | bytes 2621440
  60.0 0.0 copy-done
  60.0 0.0 copy-start.1
  60.0 0.0 copy-start.2
  60.0 0.0 copy-start.3
  60.0 1.1 %copy.19 = bf16[1,256,2560]{2,1,0:T(8,128)(2,1)} copy(bf16[1,256,2560]{2,1,0:T(8,128)(2,1)S(1)} %bitcast.9) | data formatting | bytes 2621440
  61.1 0.0 copy-done.1
  61.1 0.7 %copy.20 = bf16[1,256,256]{2,1,0:T(8,128)(2,1)} copy(bf16[1,256,256]{2,1,0:T(8,128)(2,1)S(1)} %bitcast.14) | data formatting | bytes 262144
  61.7 0.0 copy-done.2
  61.7 0.6 copy.21
  62.3 0.0 copy-done.3
  62.3 0.6 copy.22
Async XLA Ops:
  57.4 2.6 %copy-start = (bf16[256,2560]{1,0:T(8,128)(2,1)S(1)}, bf16[256,2560]{1,0:T(8,128)(2,1)}, u32[]{:S(2)}) copy-start(bf16[256,2560]{1,0:T(8,128)(2,1)} %get-tuple-element.13) | copy-start | bytes 3932164
  60.0 1.1 %copy-start.1 = (bf16[256,256]{1,0:T(8,128)(2,1)S(1)}, bf16[256,256]{1,0:T(8,128)(2,1)}, u32[]{:S(2)}) copy-start(bf16[256,256]{1,0:T(8,128)(2,1)} %get-tuple-element.14) | copy-start | bytes 393220
  60.0 1.7 %copy-start.2 = (f32[4,2560]{1,0:T(4,128)S(1)}, f32[4,2560]{1,0:T(4,128)}, u32[]{:S(2)}) copy-start(f32[4,2560]{1,0:T(4,128)} %get-tuple-element.27) | copy-start | bytes 122884
  60.0 2.3 %copy-start.3 = (f32[4,256]{1,0:T(4,128)S(1)}, f32[4,256]{1,0:T(4,128)}, u32[]{:S(2)}) copy-start(f32[4,256]{1,0:T(4,128)} %get-tuple-element.28) | copy-start | bytes 12292
